TPU v7x, 32 devices: a whole 2x2x4 slice. The times are simulated.
32 devices in a mesh: gx: 8 (over z, y), gy: 4 (over x, core).
Axes of the slice: x: 2, y: 2, z: 4, core: 2. Of those that a mesh axis runs over, the one named last changes fastest.
Arguments:
- rhs: float32 [64, 256, 256], P('gx', 'gy'), may hold values from -12 to 12
- coefs: float32 [13, 64, 256, 256], P(None, 'gx', 'gy'), may hold values from 0 to 1.4, as said below
- shifts: float32 [4], replicated, may hold values from 0.4 to 1.1
Outputs:
- basis: float32 [5, 64, 256, 256], P(None, 'gx', 'gy')
- factor: float32 [5, 5], replicated
- solution: float32 [64, 256, 256], P('gx', 'gy')
- residual: float32 [64, 256, 256], P('gx', 'gy')
Inputs may be any that keep to these rules, and one draw needn't show every extreme that they name: `coefs`: entry 0 lies in 0.6 to 1.4, entries 1 to 6 in 0.02 to 0.22, entries 7 to 12 in 0 to 0.16.
All inputs are finite; a program needn't handle non-finite values.
Results may differ from a plain program's by a relative error of at most 0.00095.
Values sent between devices are 32-bit elements; how exact they have to be, the bound alone decides.
A program may use at most 64 MiB of HBM per device.

v0:
```python
import functools

import jax
import jax.numpy as jnp
from jax import lax
from jax.experimental import pallas as pl
from jax.experimental.pallas import tpu as pltpu
from jax.sharding import PartitionSpec as P

growth = 2.0
MESH = pl.DeviceIdType.MESH
PAD = 8
ROWS = 128


def basis_kernel(
    n_gx, n_gy, shifts_hbm, rhs, coefs, v_out, w_out, gram,
    field_v, field_w, weight, part, gx_part, gy_part, shifts, y_out, y_in,
    load_sem, store_sem, xs, xr, ys, yr, gxs, gxr, gys, gyr,
):
    steps = shifts.shape[0]
    nx, ny, nz = rhs.shape
    mine = slice(1, nx + 1)
    body = slice(PAD, PAD + ny)
    gx, gy = lax.axis_index("gx"), lax.axis_index("gy")
    x_up, x_down = lax.rem(gx + 1, n_gx), lax.rem(gx + n_gx - 1, n_gx)
    has_low, has_high = gy > 0, gy < n_gy - 1

    loads = [
        pltpu.make_async_copy(rhs, field_v.at[0, mine, body, :], load_sem.at[0]),
        pltpu.make_async_copy(coefs.at[0:7], weight.at[0:7], load_sem.at[1]),
        pltpu.make_async_copy(coefs.at[7:13], weight.at[7:13], load_sem.at[2]),
        pltpu.make_async_copy(shifts_hbm, shifts, load_sem.at[3]),
    ]
    for load in loads:
        load.start()

    barrier = pltpu.get_barrier_semaphore()

    def greet_gx(d, c):
        pl.semaphore_signal(barrier, inc=1, device_id={"gx": lax.rem(gx + d, n_gx)}, device_id_type=MESH)
        return c

    def greet_gy(d, c):
        pl.semaphore_signal(barrier, inc=1, device_id={"gy": lax.rem(gy + d, n_gy)}, device_id_type=MESH)
        return c

    lax.fori_loop(1, n_gx, greet_gx, 0)
    lax.fori_loop(1, n_gy, greet_gy, 0)

    part[...] = jnp.zeros_like(part)

    def clear(fields, rows):
        for k in range(steps):
            for p in range(1, nx + 1):
                fields[k, p, rows, :] = jnp.zeros((PAD, nz), jnp.float32)

    @pl.when(jnp.logical_not(has_low))
    def _():
        clear(field_v, slice(0, PAD))
        clear(field_w, slice(0, PAD))

    @pl.when(jnp.logical_not(has_high))
    def _():
        clear(field_v, slice(PAD + ny, PAD + ny + PAD))
        clear(field_w, slice(PAD + ny, PAD + ny + PAD))

    pl.semaphore_wait(barrier, n_gx + n_gy - 2)

    chunk = ny // 4 if ny % 32 == 0 else ny
    pieces = ny // chunk
    order = [c for c in range(pieces) if 0 < c < pieces - 1] + sorted({0, pieces - 1})

    def x_copy(fields, k, which, side, c, source=None):
        slot = pieces * (2 * steps * which + 2 * k + side) + c
        rows = slice(PAD + c * chunk, PAD + (c + 1) * chunk)
        if source is None:
            source = fields.at[k, 1 if side == 0 else nx, rows, :]
        return pltpu.make_async_remote_copy(
            src_ref=source,
            dst_ref=fields.at[k, nx + 1 if side == 0 else 0, rows, :],
            send_sem=xs.at[slot],
            recv_sem=xr.at[slot],
            device_id={"gx": x_down if side == 0 else x_up},
            device_id_type=MESH,
        )

    def y_copy(k, which, side):
        slot = 2 * steps * which + 2 * k + side
        return pltpu.make_async_remote_copy(
            src_ref=y_out.at[slot],
            dst_ref=y_in.at[slot],
            send_sem=ys.at[slot],
            recv_sem=yr.at[slot],
            device_id={"gy": jnp.maximum(gy - 1, 0) if side == 0 else jnp.minimum(gy + 1, n_gy - 1)},
            device_id_type=MESH,
        )

    def y_start(fields, k, which):
        for side, there in ((0, has_low), (1, has_high)):
            slot = 2 * steps * which + 2 * k + side
            row = PAD if side == 0 else PAD + ny - 1

            @pl.when(there)
            def _():
                for p in range(nx):
                    y_out[slot, p : p + 1, :] = fields[k, p + 1, row : row + 1, :]
                y_copy(k, which, side).start()

    def y_arrived(fields, k, which):
        for side, there in ((1, has_low), (0, has_high)):
            slot = 2 * steps * which + 2 * k + side
            row = PAD + ny if side == 0 else PAD - 1

            @pl.when(there)
            def _():
                y_copy(k, which, side).wait_recv()
                for p in range(nx):
                    fields[k, p + 1, row : row + 1, :] = y_in[slot, p : p + 1, :]

    def near(fields, k, p, r, rows):
        centre = fields[k, p + 1, PAD + r : PAD + r + rows, :]
        lane = lax.broadcasted_iota(jnp.int32, centre.shape, 1)
        return centre, (
            fields[k, p, PAD + r : PAD + r + rows, :],
            fields[k, p + 2, PAD + r : PAD + r + rows, :],
            fields[k, p + 1, PAD + r - 1 : PAD + r - 1 + rows, :],
            fields[k, p + 1, PAD + r + 1 : PAD + r + 1 + rows, :],
            jnp.where(lane == 0, 0.0, pltpu.roll(centre, 1, 1)),
            jnp.where(lane == nz - 1, 0.0, pltpu.roll(centre, nz - 1, 1)),
        )

    def block_m(k, p, r, rows):
        centre, sides = near(field_v, k, p, r, rows)
        total = weight[0, p, r : r + rows, :] * centre
        for d in range(6):
            total = total + weight[1 + d, p, r : r + rows, :] * sides[d]
        field_w[k, p + 1, PAD + r : PAD + r + rows, :] = total

    def block_a(k, p, r, rows):
        centre, sides = near(field_w, k, p, r, rows)
        total = centre
        for d in range(6):
            total = total - weight[7 + d, p, r : r + rows, :] * sides[d]
        old = field_v[k, p + 1, PAD + r : PAD + r + rows, :]
        field_v[k + 1, p + 1, PAD + r : PAD + r + rows, :] = growth * (total - shifts[k] * old)

    def apply(block, fields, k, which, out, out_k, out_which, send):
        y_arrived(fields, k, which)

        def edge(p, c):
            block(k, p, 0, 8)
            block(k, p, ny - 8, 8)
            return c

        lax.fori_loop(1, nx - 1, edge, 0)

        for c in order:
            for side in range(2):
                x_copy(fields, k, which, 1 - side, c).wait_recv()
                block(k, 0 if side == 0 else nx - 1, c * chunk, chunk)

                @pl.when(send)
                def _():
                    x_copy(out, out_k, out_which, side, c).start()

        @pl.when(send)
        def _():
            y_start(out, out_k, out_which)

        def inner(p, c):
            for r in range(8, ny - 8, 16):
                block(k, p, r, min(16, ny - 8 - r))
            return c

        lax.fori_loop(1, nx - 1, inner, 0)

    def products(i):
        def one(j, c):
            def add(p, total):
                a = field_v[i, p + 1, body, :]
                b = field_v[j, p + 1, body, :]
                return total + jnp.sum((a * b).reshape(ny // 8, 8, nz), axis=0)

            total = lax.fori_loop(0, nx, add, jnp.zeros((8, nz), jnp.float32))
            row = jnp.sum(total, axis=0, keepdims=True)
            flat = row[:, :ROWS]
            for q in range(1, nz // ROWS):
                flat = flat + row[:, q * ROWS : (q + 1) * ROWS]
            part[pl.ds(i * (i + 1) // 2 + j, 1), :] = flat
            return c

        lax.fori_loop(0, i + 1, one, 0)

    for c in order:
        for side in range(2):
            plane = rhs.at[0 if side == 0 else nx - 1, c * chunk : (c + 1) * chunk, :]
            x_copy(field_v, 0, 0, side, c, plane).start()
    loads[0].wait()
    y_start(field_v, 0, 0)
    products(0)
    for load in loads[1:]:
        load.wait()

    def v_store(k):
        return pltpu.make_async_copy(field_v.at[k, mine, body, :], v_out.at[k], store_sem.at[0, k])

    def w_store(k):
        return pltpu.make_async_copy(field_w.at[k, mine, body, :], w_out.at[k], store_sem.at[1, k])

    def step(k, c):
        apply(block_m, field_v, k, 0, field_w, k, 1, k >= 0)
        w_store(k).start()
        apply(block_a, field_w, k, 1, field_v, k + 1, 0, k + 1 < steps)
        v_store(k + 1).start()
        products(k + 1)
        return c

    v_store(0).start()
    lax.fori_loop(0, steps, step, 0)

    def gather(axis, me, n, store, send_sem, recv_sem, value):
        store[me] = value

        def copy(d):
            return pltpu.make_async_remote_copy(
                src_ref=store.at[me],
                dst_ref=store.at[me],
                send_sem=send_sem.at[d],
                recv_sem=recv_sem.at[d],
                device_id={axis: lax.rem(me + d, n)},
                device_id_type=MESH,
            )

        def start(d, c):
            copy(d).start()
            return c

        def arrive(d, c):
            copy(d).wait_recv()
            return c

        def sent(d, c):
            copy(d).wait_send()
            return c

        lax.fori_loop(1, n, start, 0)
        lax.fori_loop(1, n, arrive, 0)
        total = lax.fori_loop(0, n, lambda s, t: t + store[s], jnp.zeros_like(value))
        return total, lambda: lax.fori_loop(1, n, sent, 0)

    half = part.shape[0] // 2
    sums = jnp.sum(part[...], axis=1, keepdims=True)
    left = lax.broadcasted_iota(jnp.int32, (half, ROWS), 1) < ROWS // 2
    packed = jnp.where(left, jnp.broadcast_to(sums[:half], left.shape), jnp.broadcast_to(sums[half:], left.shape))
    total, done_x = gather("gx", gx, n_gx, gx_part, gxs, gxr, packed)
    total, done_y = gather("gy", gy, n_gy, gy_part, gys, gyr, total)
    gram[0:half, :] = total
    for k in range(steps):
        gram[half + k : half + k + 1, :] = jnp.full((1, ROWS), shifts[k], jnp.float32)
    done_x()
    done_y()

    def finish(k, c):
        for which, fields in ((0, field_v), (1, field_w)):
            for side in range(2):
                for piece in range(pieces):
                    x_copy(fields, k, which, side, piece).wait_send()

            @pl.when(has_low)
            def _():
                y_copy(k, which, 0).wait_send()

            @pl.when(has_high)
            def _():
                y_copy(k, which, 1).wait_send()

        v_store(k).wait()
        w_store(k).wait()
        return c

    lax.fori_loop(0, steps, finish, 0)
    v_store(steps).wait()


def small_algebra(gram, steps, cells):
    order = steps + 1
    half = gram.shape[0] // 2
    shifts = [gram[half + k : half + k + 1, :] for k in range(steps)]
    sums = gram[:half] / cells
    turned = pltpu.roll(sums, ROWS // 2, 1)
    left = lax.broadcasted_iota(jnp.int32, sums.shape, 1) < ROWS // 2
    sums = (jnp.where(left, sums, turned), jnp.where(left, turned, sums))

    def entry(i, j):
        n = max(i, j) * (max(i, j) + 1) // 2 + min(i, j)
        return sums[n // half][n % half : n % half + 1, :]

    factor = {}
    for i in range(order):
        value = entry(i, i)
        for k in range(i):
            value = value - factor[k, i] * factor[k, i]
        factor[i, i] = jnp.sqrt(value)
        for j in range(i + 1, order):
            value = entry(i, j)
            for k in range(i):
                value = value - factor[k, i] * factor[k, j]
            factor[i, j] = value / factor[i, i]
    inverse = {}
    for j in range(order):
        inverse[j, j] = 1.0 / factor[j, j]
        for i in range(j - 1, -1, -1):
            value = factor[i, i + 1] * inverse[i + 1, j]
            for k in range(i + 2, j + 1):
                value = value + factor[i, k] * inverse[k, j]
            inverse[i, j] = -value / factor[i, i]
    zero = jnp.zeros_like(factor[0, 0])

    def upper(i, j):
        return factor.get((i, j), zero)

    hess = [[upper(i, k) * shifts[k] + upper(i, k + 1) * (1.0 / growth) for k in range(steps)] for i in range(order)]
    target = [upper(i, 0) for i in range(order)]
    for k in range(steps):
        top, below = hess[k][k], hess[k + 1][k]
        radius = jnp.sqrt(top * top + below * below)
        cosine, sine = top / radius, below / radius
        for c in range(k, steps):
            a, b = hess[k][c], hess[k + 1][c]
            hess[k][c] = cosine * a + sine * b
            hess[k + 1][c] = cosine * b - sine * a
        a, b = target[k], target[k + 1]
        target[k] = cosine * a + sine * b
        target[k + 1] = cosine * b - sine * a
    weights = [None] * steps
    for i in range(steps - 1, -1, -1):
        value = target[i]
        for k in range(i + 1, steps):
            value = value - hess[i][k] * weights[k]
        weights[i] = value / hess[i][i]
    combine = []
    for j in range(order):
        value = zero + (1.0 if j == 0 else 0.0)
        if j < steps:
            value = value - shifts[j] * weights[j]
        if j > 0:
            value = value - (1.0 / growth) * weights[j - 1]
        combine.append(value)
    return factor, inverse, weights, combine


def combine_kernel(cells, gram, v, w, basis, factor_out, solution_out, residual, table, basis_v, sol_v, res_v, sem):
    order, nx, ny, nz = v.shape
    steps = order - 1
    pairs = [(j, k) for k in range(order) for j in range(k + 1)]
    tail = len(pairs)

    factor, inverse, weights, combine = small_algebra(gram[...], steps, cells)
    values = [inverse[p] for p in pairs] + weights + combine
    for n, value in enumerate(values):
        table[n] = jnp.broadcast_to(value, table.shape[1:])
    row = lax.broadcasted_iota(jnp.int32, (8, ROWS), 0)
    column = lax.broadcasted_iota(jnp.int32, (8, ROWS), 1)
    whole = jnp.zeros((8, ROWS), jnp.float32)
    for (i, j), value in factor.items():
        whole = jnp.where((row == i) & (column == j), value, whole)
    factor_out[...] = whole[:order, :order]

    def mul(n, x):
        return table[n][None] * x

    deep = 16 if ny % 16 == 0 else 8

    def tile(p, t):
        rows = pl.ds(pl.multiple_of(t * deep, deep), deep)
        for q in range(0, nz, ROWS):
            lanes = slice(q, q + ROWS)
            load = lambda x: x.reshape(deep // 8, 8, ROWS)
            fields = [load(v[k, p, rows, lanes]) for k in range(order)]
            for k in range(order):
                total = None
                for j in range(k + 1):
                    term = mul(pairs.index((j, k)), fields[j])
                    total = term if total is None else total + term
                basis_v[k, p, rows, lanes] = total.reshape(deep, ROWS)
            total = mul(tail, load(w[0, p, rows, lanes]))
            for k in range(1, steps):
                total = total + mul(tail + k, load(w[k, p, rows, lanes]))
            sol_v[p, rows, lanes] = total.reshape(deep, ROWS)
            total = mul(tail + steps, fields[0])
            for j in range(1, order):
                total = total + mul(tail + steps + j, fields[j])
            res_v[p, rows, lanes] = total.reshape(deep, ROWS)

    def copies(p):
        return (
            pltpu.make_async_copy(basis_v.at[:, p], basis.at[:, p], sem.at[p, 0]),
            pltpu.make_async_copy(sol_v.at[p], solution_out.at[p], sem.at[p, 1]),
            pltpu.make_async_copy(res_v.at[p], residual.at[p], sem.at[p, 2]),
        )

    def plane(p, c):
        def inner(t, d):
            tile(p, t)
            return d

        lax.fori_loop(0, ny // deep, inner, 0)
        for copy in copies(p):
            copy.start()
        return c

    def finish(p, c):
        for copy in copies(p):
            copy.wait()
        return c

    lax.fori_loop(0, nx, plane, 0)
    lax.fori_loop(0, nx, finish, 0)


def device_body(n_gx, n_gy, rhs, coefs, shifts):
    steps = shifts.shape[0]
    order = steps + 1
    nx, ny, nz = rhs.shape
    f32 = jnp.float32
    grown = (nx + 2, ny + 2 * PAD, nz)
    half = -(-(order * (order + 1) // 2) // 16) * 8
    pieces = 4 if ny % 32 == 0 else 1
    hbm = pl.BlockSpec(memory_space=pltpu.HBM)
    any_space = pl.BlockSpec(memory_space=pl.ANY)
    vmem = pl.BlockSpec(memory_space=pltpu.VMEM)
    dma = pltpu.SemaphoreType.DMA
    halo = 4 * steps
    rhs = pltpu.with_memory_space_constraint(rhs, pltpu.HBM)
    coefs = pltpu.with_memory_space_constraint(coefs, pltpu.HBM)
    shifts = pltpu.with_memory_space_constraint(shifts, pltpu.HBM)
    v, w, gram = pl.pallas_call(
        functools.partial(basis_kernel, n_gx, n_gy),
        out_shape=(
            jax.ShapeDtypeStruct((order, nx, ny, nz), f32),
            jax.ShapeDtypeStruct((steps, nx, ny, nz), f32),
            jax.ShapeDtypeStruct((2 * half, ROWS), f32),
        ),
        in_specs=[hbm, hbm, hbm],
        out_specs=(any_space, any_space, vmem),
        scratch_shapes=[
            pltpu.VMEM((order,) + grown, f32),
            pltpu.VMEM((steps,) + grown, f32),
            pltpu.VMEM(coefs.shape, f32),
            pltpu.VMEM((2 * half, ROWS), f32),
            pltpu.VMEM((n_gx, half, ROWS), f32),
            pltpu.VMEM((n_gy, half, ROWS), f32),
            pltpu.SMEM(shifts.shape, f32),
            pltpu.VMEM((halo, nx, nz), f32),
            pltpu.VMEM((halo, nx, nz), f32),
            dma((4,)),
            dma((2, order)),
            dma((halo * pieces,)),
            dma((halo * pieces,)),
            dma((halo,)),
            dma((halo,)),
            dma((n_gx,)),
            dma((n_gx,)),
            dma((n_gy,)),
            dma((n_gy,)),
        ],
        compiler_params=pltpu.CompilerParams(
            collective_id=0, has_side_effects=True, vmem_limit_bytes=32 * 2**20
        ),
        name="basis",
    )(shifts, rhs, coefs)

    cells = float(nx * ny * nz * n_gx * n_gy)
    return pl.pallas_call(
        functools.partial(combine_kernel, cells),
        out_shape=(
            jax.ShapeDtypeStruct((order, nx, ny, nz), f32),
            jax.ShapeDtypeStruct((order, order), f32),
            jax.ShapeDtypeStruct((nx, ny, nz), f32),
            jax.ShapeDtypeStruct((nx, ny, nz), f32),
        ),
        in_specs=[vmem, vmem, vmem],
        out_specs=(hbm, vmem, hbm, hbm),
        scratch_shapes=[
            pltpu.VMEM((order * (order + 1) // 2 + steps + order, 8, ROWS), f32),
            pltpu.VMEM((order, nx, ny, nz), f32),
            pltpu.VMEM((nx, ny, nz), f32),
            pltpu.VMEM((nx, ny, nz), f32),
            dma((nx, 3)),
        ],
        compiler_params=pltpu.CompilerParams(vmem_limit_bytes=32 * 2**20),
        name="combine",
    )(gram, v, w)


def solution(mesh):
    placed = (P("gx", "gy", None), P(None, "gx", "gy", None), P())
    return jax.shard_map(
        functools.partial(device_body, mesh.shape["gx"], mesh.shape["gy"]),
        mesh=mesh,
        in_specs=placed,
        out_specs=(P(None, "gx", "gy", None), P(), P("gx", "gy", None), P("gx", "gy", None)),
        check_vma=False,
    )
```

profile of v0, /device:TPU:0, one launch (start us, length us, event | category | flops | bytes accessed | tf_op | source)
XLA Modules:
  0.0 53.4 jit_solution(2022885610026661142)
XLA Ops:
  0.6 49.8 %basis.1 = (f32[5,8,64,256]{3,2,1,0:T(8,128)S(1)}, f32[4,8,64,256]{3,2,1,0:T(8,128)S(1)}, f32[16,128]{1,0:T(8,128)S(1)}) custom-call(f32[4]{0:T(128)} %shifts_hbm.1, f32[8,64,256]{2,1,0:T(8,128)} %rhs.1, f32[13,8,64,256]{3,2,1,0:T(8,128)} %coefs.1), custom_call_target="tpu_custom_call" | custom-call | tf_op jit(solution)/shard_map/basis/pallas_call | solution.py:438
  50.4 2.9 %combine.1 = (f32[5,8,64,256]{3,2,1,0:T(8,128)}, f32[5,5]{1,0:T(8,128)}, f32[8,64,256]{2,1,0:T(8,128)}, f32[8,64,256]{2,1,0:T(8,128)}) custom-call(f32[16,128]{1,0:T(8,128)S(1)} %get-tuple-element.7.gram, f32[5,8,64,256]{3,2,1,0:T(8,128)S(1)} %get-tuple-element.8.v, f32[4,8,64,256]{3,2,1,0:T(8,128)S(1)} %get-tuple-element.9.w), custom_call_target="tpu_custom_call" | custom-call | tf_op jit(solution)/shard_map/combine/pallas_call | solution.py:475
where the time goes:
time: 53.5 us; the launch traced here: 53.4 us
  Pallas kernels  52.7 us (99%)
  between operations  0.64 us (1%)
    pallas_call x1, Pallas kernels, device_body(): pl.pallas_call(functools.partial(basis_kernel, n_gx, n_gy), out_shape=(ja...  49.8 us
    pallas_call x1, Pallas kernels, device_body(): pl.pallas_call(functools.partial(combine_kernel, cells), out_shape=(jax.S...  2.94 us

commit v1 on v0

v1 whole, which is shorter than its diff:
```python
import functools

import jax
import jax.numpy as jnp
from jax import lax
from jax.experimental import pallas as pl
from jax.experimental.pallas import tpu as pltpu
from jax.sharding import PartitionSpec as P

growth = 2.0
MESH = pl.DeviceIdType.MESH
PAD = 8
ROWS = 128
TILE = 8


def middle_out(count):
    low, high = (count - 1) // 2, (count - 1) // 2 + 1
    order = []
    while low >= 0 or high < count:
        if high < count:
            order.append(high)
            high += 1
        if low >= 0:
            order.append(low)
            low -= 1
    return order


def basis_kernel(
    n_gx, n_gy, shifts_hbm, rhs, coefs, fv, fw, gram,
    weight, part, peers, shifts, xout, xin, yout, yin, cout, cin,
    far, far_corner, own_row, own_corner, near_row, near_corner, far_edge,
    load_sem, xs, xr, ys, yr, cs, cr, fs, fr, gs, gr,
):
    steps = shifts.shape[0]
    order = steps + 1
    nx, ny, nz = rhs.shape
    tiles = ny // TILE
    body = slice(PAD, PAD + ny)
    face = (0, nx - 1)
    edge = (0, ny - 1)
    gx, gy = lax.axis_index("gx"), lax.axis_index("gy")
    beside_x = (lax.rem(gx + n_gx - 1, n_gx), lax.rem(gx + 1, n_gx))
    beside_y = (jnp.maximum(gy - 1, 0), jnp.minimum(gy + 1, n_gy - 1))
    there = (gy > 0, gy < n_gy - 1)
    count = n_gx * n_gy
    me = gx * n_gy + gy

    loads = [
        pltpu.make_async_copy(rhs, fv.at[0, :, body, :], load_sem.at[0]),
        pltpu.make_async_copy(coefs.at[0:7], weight.at[0:7], load_sem.at[1]),
        pltpu.make_async_copy(coefs.at[7:13], weight.at[7:13], load_sem.at[2]),
        pltpu.make_async_copy(shifts_hbm, shifts, load_sem.at[3]),
    ]
    for load in loads:
        load.start()

    cin[...] = jnp.zeros_like(cin)

    barrier = pltpu.get_barrier_semaphore()

    def peer(d):
        other = lax.rem(me + d, count)
        return {"gx": lax.div(other, n_gy), "gy": lax.rem(other, n_gy)}

    def greet(d, c):
        pl.semaphore_signal(barrier, inc=1, device_id=peer(d), device_id_type=MESH)
        return c

    lax.fori_loop(1, count, greet, 0)

    part[...] = jnp.zeros_like(part)
    blank = jnp.zeros((PAD, nz), jnp.float32)
    for fields in (fv, fw):

        def clear(p, c):
            for k in range(fields.shape[0]):
                fields[k, p, 0:PAD, :] = blank
                fields[k, p, PAD + ny : PAD + ny + PAD, :] = blank
            return c

        lax.fori_loop(0, nx, clear, 0)

    def rows_of(t):
        return slice(t * TILE, (t + 1) * TILE)

    def remote(source, target, send, receive, device):
        return pltpu.make_async_remote_copy(
            src_ref=source, dst_ref=target, send_sem=send, recv_sem=receive,
            device_id=device, device_id_type=MESH,
        )

    def x_copy(k, s, t):
        n, m = (2 * k + s) * tiles + t, (2 * k + 1 - s) * tiles + t
        return remote(
            xout.at[k, s, :, rows_of(t), :], xin.at[k, 1 - s, :, rows_of(t), :],
            xs.at[n], xr.at[m], {"gx": beside_x[s]},
        )

    def y_copy(k, s):
        return remote(
            yout.at[k, s], yin.at[k, 1 - s], ys.at[2 * k + s], yr.at[2 * k + 1 - s], {"gy": beside_y[s]}
        )

    def corner_copy(k, sx, sy):
        n, m = 4 * k + 2 * sx + sy, 4 * k + 2 * (1 - sx) + 1 - sy
        return remote(
            cout.at[n], cin.at[m], cs.at[n], cr.at[m], {"gx": beside_x[sx], "gy": beside_y[sy]}
        )

    def far_copy(s, t):
        return remote(
            weight.at[1 + s, face[s], rows_of(t), :], far.at[1 - s, rows_of(t), :],
            fs.at[s, t], fr.at[1 - s, t], {"gx": beside_x[s]},
        )

    def far_edge_copy(s):
        return remote(
            far_corner.at[s], far_edge.at[1 - s], fs.at[s, tiles], fr.at[1 - s, tiles], {"gx": beside_x[s]}
        )

    def near_copies(s):
        device = {"gy": beside_y[s]}
        return (
            remote(own_row.at[s], near_row.at[1 - s], fs.at[s, tiles + 1], fr.at[1 - s, tiles + 1], device),
            remote(own_corner.at[s], near_corner.at[1 - s], fs.at[s, tiles + 2], fr.at[1 - s, tiles + 2], device),
        )

    def along_z(centre):
        lane = lax.broadcasted_iota(jnp.int32, centre.shape, 1)
        return (
            jnp.where(lane == 0, 0.0, pltpu.roll(centre, 1, 1)),
            jnp.where(lane == nz - 1, 0.0, pltpu.roll(centre, nz - 1, 1)),
        )

    def block_m(k, p, r, rows, low=True, high=True):
        here = slice(PAD + r, PAD + r + rows)
        mine = slice(r, r + rows)
        centre = fv[k, p, here, :]
        total = weight[0, p, mine, :] * centre
        if low:
            total = total + weight[1, p, mine, :] * fv[k, p - 1, here, :]
        if high:
            total = total + weight[2, p, mine, :] * fv[k, p + 1, here, :]
        total = total + weight[3, p, mine, :] * fv[k, p, PAD + r - 1 : PAD + r - 1 + rows, :]
        total = total + weight[4, p, mine, :] * fv[k, p, PAD + r + 1 : PAD + r + 1 + rows, :]
        minus_z, plus_z = along_z(centre)
        total = total + weight[5, p, mine, :] * minus_z
        total = total + weight[6, p, mine, :] * plus_z
        fw[k, p, here, :] = total
        return total

    def block_a(k, p, r, rows, minus_x=None, plus_x=None):
        here = slice(PAD + r, PAD + r + rows)
        mine = slice(r, r + rows)
        centre = fw[k, p, here, :]
        if minus_x is None:
            minus_x = fw[k, p - 1, here, :]
        if plus_x is None:
            plus_x = fw[k, p + 1, here, :]
        total = centre - weight[7, p, mine, :] * minus_x
        total = total - weight[8, p, mine, :] * plus_x
        total = total - weight[9, p, mine, :] * fw[k, p, PAD + r - 1 : PAD + r - 1 + rows, :]
        total = total - weight[10, p, mine, :] * fw[k, p, PAD + r + 1 : PAD + r + 1 + rows, :]
        minus_z, plus_z = along_z(centre)
        total = total - weight[11, p, mine, :] * minus_z
        total = total - weight[12, p, mine, :] * plus_z
        total = growth * (total - shifts[k] * fv[k, p, here, :])
        fv[k + 1, p, here, :] = total
        return total

    def face_m(k, s, t):
        total = block_m(k, face[s], t * TILE, TILE, low=s == 1, high=s == 0)
        xout[k, s, 1, rows_of(t), :] = total

    def face_a(k, s, t):
        rows = rows_of(t)
        here = slice(PAD + t * TILE, PAD + (t + 1) * TILE)
        beyond = xin[k, s, 1, rows, :] + far[s, rows, :] * fv[k, face[s], here, :]
        if s == 0:
            total = block_a(k, 0, t * TILE, TILE, minus_x=beyond)
        else:
            total = block_a(k, nx - 1, t * TILE, TILE, plus_x=beyond)
        xout[k + 1, s, 0, rows, :] = total

    def send_corners(k):
        for sy in range(2):
            for sx in range(2):
                row = PAD + edge[sy]
                cout[4 * k + 2 * sx + sy, :, :] = fv[k, face[sx], row : row + 1, :]

            @pl.when(there[sy])
            def _():
                for sx in range(2):
                    corner_copy(k, sx, sy).start()

    def send_y(k):
        for s in range(2):
            row = PAD + edge[s]

            @pl.when(there[s])
            def _():
                for p in range(nx):
                    yout[k, s, 0, p : p + 1, :] = fv[k, p, row : row + 1, :]
                    yout[k, s, 1, p : p + 1, :] = fw[k, p, row : row + 1, :]
                y_copy(k, s).start()

    def finish_edges(k):
        for sy in range(2):

            @pl.when(there[sy])
            def _():
                for sx in range(2):
                    corner_copy(k, 1 - sx, 1 - sy).wait_recv()
                y_copy(k, 1 - sy).wait_recv()
                row = PAD + edge[sy]
                halo = PAD - 1 if sy == 0 else PAD + ny
                yin[k, sy, 1, :, :] = yin[k, sy, 1, :, :] + near_row[sy] * yout[k, sy, 0, :, :]
                yin[k, sy, 0, :, :] = own_row[sy] * yin[k, sy, 0, :, :]
                for sx in range(2):
                    p, q = face[sx], edge[sy]
                    line = cin[4 * k + 2 * sx + sy, :, :]
                    yin[k, sy, 1, p : p + 1, :] = yin[k, sy, 1, p : p + 1, :] + near_corner[sy, sx : sx + 1, :] * line
                    xin[k, sx, 1, q : q + 1, :] = xin[k, sx, 1, q : q + 1, :] + far_edge[sx, sy : sy + 1, :] * line
                for p in range(nx):
                    fw[k, p, halo : halo + 1, :] = yin[k, sy, 1, p : p + 1, :]
                    fw[k, p, row : row + 1, :] = fw[k, p, row : row + 1, :] + yin[k, sy, 0, p : p + 1, :]

    def products(i):
        def one(j, c):
            def add(p, total):
                a = fv[i, p, body, :]
                b = fv[j, p, body, :]
                return total + jnp.sum((a * b).reshape(ny // 8, 8, nz), axis=0)

            keep(i * (i + 1) // 2 + j, lax.fori_loop(0, nx, add, jnp.zeros((8, nz), jnp.float32)))
            return c

        lax.fori_loop(0, i + 1, one, 0)

    def keep(n, total):
        row = jnp.sum(total, axis=0, keepdims=True)
        flat = row[:, :ROWS]
        for q in range(1, nz // ROWS):
            flat = flat + row[:, q * ROWS : (q + 1) * ROWS]
        part[pl.ds(n, 1), :] = flat

    def last_products():
        def add(p, totals):
            a = fv[steps, p, body, :]
            return tuple(
                total + jnp.sum((a * fv[j, p, body, :]).reshape(ny // 8, 8, nz), axis=0)
                for j, total in enumerate(totals)
            )

        totals = lax.fori_loop(0, nx, add, tuple(jnp.zeros((8, nz), jnp.float32) for _ in range(order)))
        for j, total in enumerate(totals):
            keep(steps * (steps + 1) // 2 + j, total)

    def inner_rows():
        return [(r, min(16, ny - TILE - r)) for r in range(TILE, ny - TILE, 16)]

    def inner_m(k):
        def one(p, c):
            for r, rows in inner_rows():
                block_m(k, p, r, rows)
            return c

        lax.fori_loop(1, nx - 1, one, 0)

    def inner_a(k):
        def one(p, c):
            for r, rows in inner_rows():
                block_a(k, p, r, rows)
            return c

        lax.fori_loop(2, nx - 2, one, 0)

    def edge_m(k):
        def one(p, c):
            block_m(k, p, 0, TILE)
            block_m(k, p, ny - TILE, TILE)
            return c

        lax.fori_loop(1, nx - 1, one, 0)

    def edge_a(k):
        def one(p, c):
            block_a(k, p, 0, TILE)
            block_a(k, p, ny - TILE, TILE)
            return c

        lax.fori_loop(2, nx - 2, one, 0)

    sequence = middle_out(tiles)

    loads[0].wait()
    for s in range(2):
        xout[0, s, 0, :, :] = fv[0, face[s], body, :]
    loads[1].wait()
    for t in sequence:
        for s in range(2):
            face_m(0, s, t)
    edge_m(0)
    for s in range(2):
        r = edge[s]
        for p in range(nx):
            own_row[s, p : p + 1, :] = weight[3 + s, p, r : r + 1, :]
        for sx in range(2):
            own_corner[s, sx : sx + 1, :] = weight[1 + sx, face[sx], r : r + 1, :]
        for sy in range(2):
            far_corner[s, sy : sy + 1, :] = weight[3 + sy, face[s], edge[sy] : edge[sy] + 1, :]
    pl.semaphore_wait(barrier, count - 1)
    for s in range(2):
        far_edge_copy(s).start()
    send_corners(0)
    for t in sequence:
        for s in range(2):
            x_copy(0, s, t).start()
            far_copy(s, t).start()
    for s in range(2):

        @pl.when(there[s])
        def _():
            for copy in near_copies(s):
                copy.start()

    send_y(0)
    inner_m(0)
    loads[2].wait()
    loads[3].wait()

    def step(k, send):
        inner_a(k)
        products(k)
        arrived, final, drafted = set(), set(), set()

        def needs(u):
            return {q for q in (u - 1, u, u + 1) if 0 <= q < tiles}

        for t in sequence:
            for s in range(2):
                x_copy(k, 1 - s, t).wait_recv()

                @pl.when(k == 0)
                def _():
                    far_copy(1 - s, t).wait_recv()

                here = slice(PAD + t * TILE, PAD + (t + 1) * TILE)
                fw[k, face[s], here, :] = (
                    fw[k, face[s], here, :] + weight[1 + s, face[s], rows_of(t), :] * xin[k, s, 0, rows_of(t), :]
                )
            arrived.add(t)
            last = len(arrived) == tiles
            if last:

                @pl.when(k == 0)
                def _():
                    for s in range(2):
                        far_edge_copy(1 - s).wait_recv()

                        @pl.when(there[s])
                        def _():
                            for copy in near_copies(1 - s):
                                copy.wait_recv()

                finish_edges(k)
            ready = [
                u for u in sequence
                if u not in final and needs(u) <= arrived and (last or 0 < u < tiles - 1)
            ]
            for u in ready:
                final.add(u)
            extra = sorted(set().union(*[needs(u) for u in ready]) - final) if send and ready else []
            for u in ready + extra:
                for s in range(2):
                    face_a(k, s, u)
            for u in ready:
                block_a(k, 1, u * TILE, TILE)
                block_a(k, nx - 2, u * TILE, TILE)
            if send:
                if last:
                    send_corners(k + 1)
                for u in ready:
                    for s in range(2):
                        face_m(k + 1, s, u)
                        x_copy(k + 1, s, u).start()
        edge_a(k)
        if send:
            edge_m(k + 1)
            send_y(k + 1)
            inner_m(k + 1)

    def looped(k, c):
        step(k, True)
        return c

    lax.fori_loop(0, steps - 1, looped, 0)
    step(steps - 1, False)
    last_products()

    height = part.shape[0]
    row = lax.broadcasted_iota(jnp.int32, (height, ROWS), 0)
    lane = lax.broadcasted_iota(jnp.int32, (height, ROWS), 1)
    sums = jnp.sum(part[...], axis=1, keepdims=True)
    packed = jnp.sum(jnp.where(row == lane, jnp.broadcast_to(sums, row.shape), 0.0), axis=0, keepdims=True)
    peers[pl.ds(me, 1), :] = packed

    def peer_copy(d):
        return remote(peers.at[pl.ds(me, 1), :], peers.at[pl.ds(me, 1), :], gs.at[d], gr.at[d], peer(d))

    def peer_start(d, c):
        peer_copy(d).start()
        return c

    def peer_arrive(d, c):
        peer_copy(d).wait_recv()
        return c

    def peer_sent(d, c):
        peer_copy(d).wait_send()
        return c

    lax.fori_loop(1, count, peer_start, 0)

    def sent(k, c):
        for s in range(2):
            for t in range(tiles):
                x_copy(k, s, t).wait_send()

            @pl.when(there[s])
            def _():
                y_copy(k, s).wait_send()
                for sx in range(2):
                    corner_copy(k, sx, s).wait_send()

        return c

    lax.fori_loop(0, steps, sent, 0)
    for s in range(2):
        for t in range(tiles):
            far_copy(s, t).wait_send()
        far_edge_copy(s).wait_send()

        @pl.when(there[s])
        def _():
            for copy in near_copies(s):
                copy.wait_send()

    lax.fori_loop(1, count, peer_arrive, 0)
    total = jnp.sum(peers[...], axis=0, keepdims=True)
    spread = jnp.sum(jnp.where(row == lane, jnp.broadcast_to(total, row.shape), 0.0), axis=1, keepdims=True)
    gram[0:height, :] = jnp.broadcast_to(spread, row.shape)
    for k in range(steps):
        gram[height + k : height + k + 1, :] = jnp.full((1, ROWS), shifts[k], jnp.float32)
    lax.fori_loop(1, count, peer_sent, 0)


def small_algebra(gram, steps, cells):
    order = steps + 1
    height = -(-(order * (order + 1) // 2) // 8) * 8
    shifts = [gram[height + k : height + k + 1, :] for k in range(steps)]
    sums = gram[:height] / cells

    def entry(i, j):
        n = max(i, j) * (max(i, j) + 1) // 2 + min(i, j)
        return sums[n : n + 1, :]

    factor = {}
    for i in range(order):
        value = entry(i, i)
        for k in range(i):
            value = value - factor[k, i] * factor[k, i]
        factor[i, i] = jnp.sqrt(value)
        for j in range(i + 1, order):
            value = entry(i, j)
            for k in range(i):
                value = value - factor[k, i] * factor[k, j]
            factor[i, j] = value / factor[i, i]
    inverse = {}
    for j in range(order):
        inverse[j, j] = 1.0 / factor[j, j]
        for i in range(j - 1, -1, -1):
            value = factor[i, i + 1] * inverse[i + 1, j]
            for k in range(i + 2, j + 1):
                value = value + factor[i, k] * inverse[k, j]
            inverse[i, j] = -value / factor[i, i]
    zero = jnp.zeros_like(factor[0, 0])

    def upper(i, j):
        return factor.get((i, j), zero)

    hess = [[upper(i, k) * shifts[k] + upper(i, k + 1) * (1.0 / growth) for k in range(steps)] for i in range(order)]
    target = [upper(i, 0) for i in range(order)]
    for k in range(steps):
        top, below = hess[k][k], hess[k + 1][k]
        radius = jnp.sqrt(top * top + below * below)
        cosine, sine = top / radius, below / radius
        for c in range(k, steps):
            a, b = hess[k][c], hess[k + 1][c]
            hess[k][c] = cosine * a + sine * b
            hess[k + 1][c] = cosine * b - sine * a
        a, b = target[k], target[k + 1]
        target[k] = cosine * a + sine * b
        target[k + 1] = cosine * b - sine * a
    weights = [None] * steps
    for i in range(steps - 1, -1, -1):
        value = target[i]
        for k in range(i + 1, steps):
            value = value - hess[i][k] * weights[k]
        weights[i] = value / hess[i][i]
    combine = []
    for j in range(order):
        value = zero + (1.0 if j == 0 else 0.0)
        if j < steps:
            value = value - shifts[j] * weights[j]
        if j > 0:
            value = value - (1.0 / growth) * weights[j - 1]
        combine.append(value)
    return factor, inverse, weights, combine


def combine_kernel(cells, gram, v, w, basis, factor_out, solution_out, residual, table, basis_v, sol_v, res_v, sem):
    order, nx, ny, nz = basis_v.shape
    steps = order - 1
    pairs = [(j, k) for k in range(order) for j in range(k + 1)]
    tail = len(pairs)

    factor, inverse, weights, combine = small_algebra(gram[...], steps, cells)
    values = [inverse[p] for p in pairs] + weights + combine
    for n, value in enumerate(values):
        table[n] = jnp.broadcast_to(value, table.shape[1:])
    row = lax.broadcasted_iota(jnp.int32, (8, ROWS), 0)
    column = lax.broadcasted_iota(jnp.int32, (8, ROWS), 1)
    whole = jnp.zeros((8, ROWS), jnp.float32)
    for (i, j), value in factor.items():
        whole = jnp.where((row == i) & (column == j), value, whole)
    factor_out[...] = whole[:order, :order]

    def mul(n, x):
        return table[n][None] * x

    deep = 16 if ny % 16 == 0 else 8

    def tile(p, t):
        rows = pl.ds(pl.multiple_of(t * deep, deep), deep)
        for q in range(0, nz, ROWS):
            lanes = slice(q, q + ROWS)
            load = lambda x: x.reshape(deep // 8, 8, ROWS)
            padded = pl.ds(pl.multiple_of(PAD + t * deep, 8), deep)
            fields = [load(v[k, p, padded, lanes]) for k in range(order)]
            for k in range(order):
                total = None
                for j in range(k + 1):
                    term = mul(pairs.index((j, k)), fields[j])
                    total = term if total is None else total + term
                basis_v[k, p, rows, lanes] = total.reshape(deep, ROWS)
            total = mul(tail, load(w[0, p, padded, lanes]))
            for k in range(1, steps):
                total = total + mul(tail + k, load(w[k, p, padded, lanes]))
            sol_v[p, rows, lanes] = total.reshape(deep, ROWS)
            total = mul(tail + steps, fields[0])
            for j in range(1, order):
                total = total + mul(tail + steps + j, fields[j])
            res_v[p, rows, lanes] = total.reshape(deep, ROWS)

    def copies(p):
        return (
            pltpu.make_async_copy(basis_v.at[:, p], basis.at[:, p], sem.at[p, 0]),
            pltpu.make_async_copy(sol_v.at[p], solution_out.at[p], sem.at[p, 1]),
            pltpu.make_async_copy(res_v.at[p], residual.at[p], sem.at[p, 2]),
        )

    def plane(p, c):
        def inner(t, d):
            tile(p, t)
            return d

        lax.fori_loop(0, ny // deep, inner, 0)
        for copy in copies(p):
            copy.start()
        return c

    def finish(p, c):
        for copy in copies(p):
            copy.wait()
        return c

    lax.fori_loop(0, nx, plane, 0)
    lax.fori_loop(0, nx, finish, 0)


def device_body(n_gx, n_gy, rhs, coefs, shifts):
    steps = shifts.shape[0]
    order = steps + 1
    nx, ny, nz = rhs.shape
    f32 = jnp.float32
    grown = (nx, ny + 2 * PAD, nz)
    height = -(-(order * (order + 1) // 2) // 8) * 8
    gram_rows = height + -(-steps // 8) * 8
    tiles = ny // TILE
    hbm = pl.BlockSpec(memory_space=pltpu.HBM)
    vmem = pl.BlockSpec(memory_space=pltpu.VMEM)
    dma = pltpu.SemaphoreType.DMA
    rhs = pltpu.with_memory_space_constraint(rhs, pltpu.HBM)
    coefs = pltpu.with_memory_space_constraint(coefs, pltpu.HBM)
    shifts = pltpu.with_memory_space_constraint(shifts, pltpu.HBM)
    v, w, gram = pl.pallas_call(
        functools.partial(basis_kernel, n_gx, n_gy),
        out_shape=(
            jax.ShapeDtypeStruct((order,) + grown, f32),
            jax.ShapeDtypeStruct((steps,) + grown, f32),
            jax.ShapeDtypeStruct((gram_rows, ROWS), f32),
        ),
        in_specs=[hbm, hbm, hbm],
        out_specs=(vmem, vmem, vmem),
        scratch_shapes=[
            pltpu.VMEM(coefs.shape, f32),
            pltpu.VMEM((height, ROWS), f32),
            pltpu.VMEM((n_gx * n_gy, ROWS), f32),
            pltpu.SMEM(shifts.shape, f32),
            pltpu.VMEM((order, 2, 2, ny, nz), f32),
            pltpu.VMEM((steps, 2, 2, ny, nz), f32),
            pltpu.VMEM((order, 2, 2, nx, nz), f32),
            pltpu.VMEM((steps, 2, 2, nx, nz), f32),
            pltpu.VMEM((4 * order, 1, nz), f32),
            pltpu.VMEM((4 * steps, 1, nz), f32),
            pltpu.VMEM((2, ny, nz), f32),
            pltpu.VMEM((2, 2, nz), f32),
            pltpu.VMEM((2, nx, nz), f32),
            pltpu.VMEM((2, 2, nz), f32),
            pltpu.VMEM((2, nx, nz), f32),
            pltpu.VMEM((2, 2, nz), f32),
            pltpu.VMEM((2, 2, nz), f32),
            dma((4,)),
            dma((2 * steps * tiles,)),
            dma((2 * steps * tiles,)),
            dma((2 * steps,)),
            dma((2 * steps,)),
            dma((4 * steps,)),
            dma((4 * steps,)),
            dma((2, tiles + 3)),
            dma((2, tiles + 3)),
            dma((n_gx * n_gy,)),
            dma((n_gx * n_gy,)),
        ],
        compiler_params=pltpu.CompilerParams(
            collective_id=0, has_side_effects=True, vmem_limit_bytes=32 * 2**20
        ),
        name="basis",
    )(shifts, rhs, coefs)

    cells = float(nx * ny * nz * n_gx * n_gy)
    return pl.pallas_call(
        functools.partial(combine_kernel, cells),
        out_shape=(
            jax.ShapeDtypeStruct((order, nx, ny, nz), f32),
            jax.ShapeDtypeStruct((order, order), f32),
            jax.ShapeDtypeStruct((nx, ny, nz), f32),
            jax.ShapeDtypeStruct((nx, ny, nz), f32),
        ),
        in_specs=[vmem, vmem, vmem],
        out_specs=(hbm, vmem, hbm, hbm),
        scratch_shapes=[
            pltpu.VMEM((order * (order + 1) // 2 + steps + order, 8, ROWS), f32),
            pltpu.VMEM((order, nx, ny, nz), f32),
            pltpu.VMEM((nx, ny, nz), f32),
            pltpu.VMEM((nx, ny, nz), f32),
            dma((nx, 3)),
        ],
        compiler_params=pltpu.CompilerParams(vmem_limit_bytes=32 * 2**20),
        name="combine",
    )(gram, v, w)


def solution(mesh):
    placed = (P("gx", "gy", None), P(None, "gx", "gy", None), P())
    return jax.shard_map(
        functools.partial(device_body, mesh.shape["gx"], mesh.shape["gy"]),
        mesh=mesh,
        in_specs=placed,
        out_specs=(P(None, "gx", "gy", None), P(), P("gx", "gy", None), P("gx", "gy", None)),
        check_vma=False,
    )
```

time: 53.5 us -> 47.1 us (0.88)
  Pallas kernels: 52.7 us -> 46.4 us
    pallas_call x1, Pallas kernels: 49.8 us -> 43.5 us  [device_body(): pl.pallas_call(functools.partial(basis_kernel, n_gx, n_gy), out_shape=(ja...]
where the time goes in v1:
time: 47.1 us; the launch traced here: 47 us
  Pallas kernels  46.4 us (99%)
  between operations  0.64 us (1%)
    pallas_call x1, Pallas kernels, device_body(): pl.pallas_call(functools.partial(basis_kernel, n_gx, n_gy), out_shape=(ja...  43.5 us
    pallas_call x1, Pallas kernels, device_body(): pl.pallas_call(functools.partial(combine_kernel, cells), out_shape=(jax.S...  2.87 us

profile of v1, /device:TPU:0, one launch (start us, length us, event | category | flops | bytes accessed | tf_op | source)
XLA Modules:
  0.0 47.0 jit_solution(6030943658147156938)
XLA Ops:
  0.6 43.5 %basis.1 = (f32[5,8,80,256]{3,2,1,0:T(8,128)S(1)}, f32[4,8,80,256]{3,2,1,0:T(8,128)S(1)}, f32[24,128]{1,0:T(8,128)S(1)}) custom-call(f32[4]{0:T(128)} %shifts_hbm.1, f32[8,64,256]{2,1,0:T(8,128)} %rhs.1, f32[13,8,64,256]{3,2,1,0:T(8,128)} %coefs.1), custom_call_target="tpu_custom_call" | custom-call | tf_op jit(solution)/shard_map/basis/pallas_call | solution.py:609
  44.1 2.9 %combine.1 = (f32[5,8,64,256]{3,2,1,0:T(8,128)}, f32[5,5]{1,0:T(8,128)}, f32[8,64,256]{2,1,0:T(8,128)}, f32[8,64,256]{2,1,0:T(8,128)}) custom-call(f32[24,128]{1,0:T(8,128)S(1)} %get-tuple-element.7.gram, f32[5,8,80,256]{3,2,1,0:T(8,128)S(1)} %get-tuple-element.8.v, f32[4,8,80,256]{3,2,1,0:T(8,128)S(1)} %get-tuple-element.9.w), custom_call_target="tpu_custom_call" | custom-call | tf_op jit(solution)/shard_map/combine/pallas_call | solution.py:655

commit v2 on v1

--- a/solution.py
+++ b/solution.py
@@ -29,9 +29,9 @@
 
 def basis_kernel(
     n_gx, n_gy, shifts_hbm, rhs, coefs, fv, fw, gram,
-    weight, part, peers, shifts, xout, xin, yout, yin, cout, cin,
+    weight, part, sums, peers, shifts, xout, xin, yout, yin, cout, cin,
     far, far_corner, own_row, own_corner, near_row, near_corner, far_edge,
-    load_sem, xs, xr, ys, yr, cs, cr, fs, fr, gs, gr,
+    load_sem, hello, xs, xr, ys, yr, cs, cr, fs, fr, gs, gr,
 ):
     steps = shifts.shape[0]
     order = steps + 1
@@ -49,9 +49,11 @@
 
     loads = [
         pltpu.make_async_copy(rhs, fv.at[0, :, body, :], load_sem.at[0]),
-        pltpu.make_async_copy(coefs.at[0:7], weight.at[0:7], load_sem.at[1]),
-        pltpu.make_async_copy(coefs.at[7:13], weight.at[7:13], load_sem.at[2]),
-        pltpu.make_async_copy(shifts_hbm, shifts, load_sem.at[3]),
+        pltpu.make_async_copy(coefs.at[0:7, 0], weight.at[0:7, 0], load_sem.at[1]),
+        pltpu.make_async_copy(coefs.at[0:7, nx - 1], weight.at[0:7, nx - 1], load_sem.at[2]),
+        pltpu.make_async_copy(coefs.at[0:7, 1 : nx - 1], weight.at[0:7, 1 : nx - 1], load_sem.at[3]),
+        pltpu.make_async_copy(coefs.at[7:13], weight.at[7:13], load_sem.at[4]),
+        pltpu.make_async_copy(shifts_hbm, shifts, load_sem.at[5]),
     ]
     for load in loads:
         load.start()
@@ -64,11 +66,37 @@
         other = lax.rem(me + d, count)
         return {"gx": lax.div(other, n_gy), "gy": lax.rem(other, n_gy)}
 
-    def greet(d, c):
-        pl.semaphore_signal(barrier, inc=1, device_id=peer(d), device_id_type=MESH)
-        return c
-
-    lax.fori_loop(1, count, greet, 0)
+    def greet(device):
+        pl.semaphore_signal(barrier, inc=1, device_id=device, device_id_type=MESH)
+
+    for x in beside_x:
+        greet({"gx": x})
+    for s in range(2):
+
+        @pl.when(there[s])
+        def _():
+            greet({"gy": beside_y[s]})
+            for x in beside_x:
+                greet({"gx": x, "gy": beside_y[s]})
+
+    greet(peer(1))
+    greet(peer(count - 1))
+    greetings = 4 + 3 * (there[0].astype(jnp.int32) + there[1].astype(jnp.int32))
+
+    strides = []
+    while (2 ** len(strides)) * 2 < count:
+        strides.append(2 ** len(strides))
+
+    def hello_signal(r):
+        for d in (strides[r], count - strides[r]):
+            pl.semaphore_signal(hello.at[r], inc=1, device_id=peer(d), device_id_type=MESH)
+
+    def hello_rounds(k):
+        share = -(-len(strides) // steps)
+        for r in range(k * share, min((k + 1) * share, len(strides))):
+            pl.semaphore_wait(hello.at[r], 2)
+            if r + 1 < len(strides):
+                hello_signal(r + 1)
 
     part[...] = jnp.zeros_like(part)
     blank = jnp.zeros((PAD, nz), jnp.float32)
@@ -93,8 +121,9 @@
 
     def x_copy(k, s, t):
         n, m = (2 * k + s) * tiles + t, (2 * k + 1 - s) * tiles + t
+        kinds = slice(1 if k == 0 else 0, 2)
         return remote(
-            xout.at[k, s, :, rows_of(t), :], xin.at[k, 1 - s, :, rows_of(t), :],
+            xout.at[k, s, kinds, rows_of(t), :], xin.at[k, 1 - s, kinds, rows_of(t), :],
             xs.at[n], xr.at[m], {"gx": beside_x[s]},
         )
 
@@ -109,9 +138,14 @@
             cout.at[n], cin.at[m], cs.at[n], cr.at[m], {"gx": beside_x[sx], "gy": beside_y[sy]}
         )
 
+    def first_copy(s):
+        return remote(
+            rhs.at[face[s]], xin.at[0, 1 - s, 0], fs.at[s, tiles + 3], fr.at[1 - s, tiles + 3], {"gx": beside_x[s]}
+        )
+
     def far_copy(s, t):
         return remote(
-            weight.at[1 + s, face[s], rows_of(t), :], far.at[1 - s, rows_of(t), :],
+            coefs.at[1 + s, face[s], rows_of(t), :], far.at[1 - s, rows_of(t), :],
             fs.at[s, t], fr.at[1 - s, t], {"gx": beside_x[s]},
         )
 
@@ -184,16 +218,20 @@
             total = block_a(k, nx - 1, t * TILE, TILE, plus_x=beyond)
         xout[k + 1, s, 0, rows, :] = total
 
+    def start_corners(k):
+        for sy in range(2):
+
+            @pl.when(there[sy])
+            def _():
+                for sx in range(2):
+                    corner_copy(k, sx, sy).start()
+
     def send_corners(k):
         for sy in range(2):
             for sx in range(2):
                 row = PAD + edge[sy]
                 cout[4 * k + 2 * sx + sy, :, :] = fv[k, face[sx], row : row + 1, :]
-
-            @pl.when(there[sy])
-            def _():
-                for sx in range(2):
-                    corner_copy(k, sx, sy).start()
+        start_corners(k)
 
     def send_y(k):
         for s in range(2):
@@ -227,36 +265,30 @@
                     fw[k, p, halo : halo + 1, :] = yin[k, sy, 1, p : p + 1, :]
                     fw[k, p, row : row + 1, :] = fw[k, p, row : row + 1, :] + yin[k, sy, 0, p : p + 1, :]
 
-    def products(i):
-        def one(j, c):
-            def add(p, total):
-                a = fv[i, p, body, :]
-                b = fv[j, p, body, :]
-                return total + jnp.sum((a * b).reshape(ny // 8, 8, nz), axis=0)
-
-            keep(i * (i + 1) // 2 + j, lax.fori_loop(0, nx, add, jnp.zeros((8, nz), jnp.float32)))
-            return c
-
-        lax.fori_loop(0, i + 1, one, 0)
-
-    def keep(n, total):
-        row = jnp.sum(total, axis=0, keepdims=True)
-        flat = row[:, :ROWS]
-        for q in range(1, nz // ROWS):
-            flat = flat + row[:, q * ROWS : (q + 1) * ROWS]
-        part[pl.ds(n, 1), :] = flat
-
-    def last_products():
+    def products(i, planes, start, size):
         def add(p, totals):
-            a = fv[steps, p, body, :]
+            a = fv[i, p, pl.ds(PAD + start, size), :]
             return tuple(
-                total + jnp.sum((a * fv[j, p, body, :]).reshape(ny // 8, 8, nz), axis=0)
+                total + jnp.sum((a * fv[j, p, pl.ds(PAD + start, size), :]).reshape(size // 8, 8, nz), axis=0)
                 for j, total in enumerate(totals)
             )
 
-        totals = lax.fori_loop(0, nx, add, tuple(jnp.zeros((8, nz), jnp.float32) for _ in range(order)))
+        totals = lax.fori_loop(*planes, add, tuple(sums[j] for j in range(i + 1)))
         for j, total in enumerate(totals):
-            keep(steps * (steps + 1) // 2 + j, total)
+            sums[j, :, :] = total
+
+    def forget(i):
+        for j in range(i + 1):
+            sums[j, :, :] = jnp.zeros((8, nz), jnp.float32)
+
+    def keep(i):
+        for j in range(i + 1):
+            row = jnp.sum(sums[j], axis=0, keepdims=True)
+            flat = row[:, :ROWS]
+            for q in range(1, nz // ROWS):
+                flat = flat + row[:, q * ROWS : (q + 1) * ROWS]
+            n = i * (i + 1) // 2 + j
+            part[n : n + 1, :] = flat
 
     def inner_rows():
         return [(r, min(16, ny - TILE - r)) for r in range(TILE, ny - TILE, 16)]
@@ -296,44 +328,57 @@
     sequence = middle_out(tiles)
 
     loads[0].wait()
+    for sy in range(2):
+        for sx in range(2):
+            row = PAD + edge[sy]
+            cout[2 * sx + sy, :, :] = fv[0, face[sx], row : row + 1, :]
+    pl.semaphore_wait(barrier, greetings)
     for s in range(2):
-        xout[0, s, 0, :, :] = fv[0, face[s], body, :]
+        first_copy(s).start()
+    start_corners(0)
+    if strides:
+        hello_signal(0)
     loads[1].wait()
+    loads[2].wait()
     for t in sequence:
         for s in range(2):
             face_m(0, s, t)
-    edge_m(0)
+            x_copy(0, s, t).start()
+            far_copy(s, t).start()
+    loads[3].wait()
     for s in range(2):
         r = edge[s]
+        for sy in range(2):
+            far_corner[s, sy : sy + 1, :] = weight[3 + sy, face[s], edge[sy] : edge[sy] + 1, :]
+        far_edge_copy(s).start()
         for p in range(nx):
             own_row[s, p : p + 1, :] = weight[3 + s, p, r : r + 1, :]
         for sx in range(2):
             own_corner[s, sx : sx + 1, :] = weight[1 + sx, face[sx], r : r + 1, :]
-        for sy in range(2):
-            far_corner[s, sy : sy + 1, :] = weight[3 + sy, face[s], edge[sy] : edge[sy] + 1, :]
-    pl.semaphore_wait(barrier, count - 1)
-    for s in range(2):
-        far_edge_copy(s).start()
-    send_corners(0)
-    for t in sequence:
-        for s in range(2):
-            x_copy(0, s, t).start()
-            far_copy(s, t).start()
-    for s in range(2):
 
         @pl.when(there[s])
         def _():
             for copy in near_copies(s):
                 copy.start()
 
+    edge_m(0)
     send_y(0)
     inner_m(0)
-    loads[2].wait()
-    loads[3].wait()
+    loads[4].wait()
+    loads[5].wait()
 
     def step(k, send):
         inner_a(k)
-        products(k)
+        forget(k)
+        products(k, (0, nx), 0, ny)
+        keep(k)
+        hello_rounds(k)
+        if not send:
+            forget(k + 1)
+            products(k + 1, (2, nx - 2), TILE, ny - 2 * TILE)
+        if k == 0:
+            for s in range(2):
+                first_copy(1 - s).wait_recv()
         arrived, final, drafted = set(), set(), set()
 
         def needs(u):
@@ -342,9 +387,7 @@
         for t in sequence:
             for s in range(2):
                 x_copy(k, 1 - s, t).wait_recv()
-
-                @pl.when(k == 0)
-                def _():
+                if k == 0:
                     far_copy(1 - s, t).wait_recv()
 
                 here = slice(PAD + t * TILE, PAD + (t + 1) * TILE)
@@ -354,9 +397,7 @@
             arrived.add(t)
             last = len(arrived) == tiles
             if last:
-
-                @pl.when(k == 0)
-                def _():
+                if k == 0:
                     for s in range(2):
                         far_edge_copy(1 - s).wait_recv()
 
@@ -392,19 +433,19 @@
             send_y(k + 1)
             inner_m(k + 1)
 
-    def looped(k, c):
-        step(k, True)
-        return c
-
-    lax.fori_loop(0, steps - 1, looped, 0)
-    step(steps - 1, False)
-    last_products()
+    for k in range(steps):
+        step(k, k + 1 < steps)
+    products(steps, (2, nx - 2), 0, TILE)
+    products(steps, (2, nx - 2), ny - TILE, TILE)
+    products(steps, (0, 2), 0, ny)
+    products(steps, (nx - 2, nx), 0, ny)
+    keep(steps)
 
     height = part.shape[0]
     row = lax.broadcasted_iota(jnp.int32, (height, ROWS), 0)
     lane = lax.broadcasted_iota(jnp.int32, (height, ROWS), 1)
-    sums = jnp.sum(part[...], axis=1, keepdims=True)
-    packed = jnp.sum(jnp.where(row == lane, jnp.broadcast_to(sums, row.shape), 0.0), axis=0, keepdims=True)
+    column = jnp.sum(part[...], axis=1, keepdims=True)
+    packed = jnp.sum(jnp.where(row == lane, jnp.broadcast_to(column, row.shape), 0.0), axis=0, keepdims=True)
     peers[pl.ds(me, 1), :] = packed
 
     def peer_copy(d):
@@ -424,7 +465,7 @@
 
     lax.fori_loop(1, count, peer_start, 0)
 
-    def sent(k, c):
+    for k in range(steps):
         for s in range(2):
             for t in range(tiles):
                 x_copy(k, s, t).wait_send()
@@ -435,10 +476,8 @@
                 for sx in range(2):
                     corner_copy(k, sx, s).wait_send()
 
-        return c
-
-    lax.fori_loop(0, steps, sent, 0)
     for s in range(2):
+        first_copy(s).wait_send()
         for t in range(tiles):
             far_copy(s, t).wait_send()
         far_edge_copy(s).wait_send()
@@ -618,6 +657,7 @@
         scratch_shapes=[
             pltpu.VMEM(coefs.shape, f32),
             pltpu.VMEM((height, ROWS), f32),
+            pltpu.VMEM((order, 8, nz), f32),
             pltpu.VMEM((n_gx * n_gy, ROWS), f32),
             pltpu.SMEM(shifts.shape, f32),
             pltpu.VMEM((order, 2, 2, ny, nz), f32),
@@ -633,15 +673,16 @@
             pltpu.VMEM((2, nx, nz), f32),
             pltpu.VMEM((2, 2, nz), f32),
             pltpu.VMEM((2, 2, nz), f32),
-            dma((4,)),
+            dma((6,)),
+            pltpu.SemaphoreType.REGULAR((16,)),
             dma((2 * steps * tiles,)),
             dma((2 * steps * tiles,)),
             dma((2 * steps,)),
             dma((2 * steps,)),
             dma((4 * steps,)),
             dma((4 * steps,)),
-            dma((2, tiles + 3)),
-            dma((2, tiles + 3)),
+            dma((2, tiles + 4)),
+            dma((2, tiles + 4)),
             dma((n_gx * n_gy,)),
             dma((n_gx * n_gy,)),
         ],

time: 47.1 us -> 45.9 us (0.975)
  Pallas kernels: 46.4 us -> 45.1 us
    pallas_call x1, Pallas kernels: 43.5 us -> 42.2 us  [device_body(): pl.pallas_call(functools.partial(basis_kernel, n_gx, n_gy), out_shape=(ja...]
where the time goes in v2:
time: 45.9 us; the launch traced here: 45.7 us
  Pallas kernels  45.1 us (98%)
  between operations  0.64 us (1%)
    pallas_call x1, Pallas kernels, device_body(): pl.pallas_call(functools.partial(basis_kernel, n_gx, n_gy), out_shape=(ja...  42.2 us
    pallas_call x1, Pallas kernels, device_body(): pl.pallas_call(functools.partial(combine_kernel, cells), out_shape=(jax.S...  2.87 us

profile of v2, /device:TPU:0, one launch (start us, length us, event | category | flops | bytes accessed | tf_op | source)
XLA Modules:
  0.0 45.7 jit_solution(10147160439096187793)
XLA Ops:
  0.6 42.2 %basis.1 = (f32[5,8,80,256]{3,2,1,0:T(8,128)S(1)}, f32[4,8,80,256]{3,2,1,0:T(8,128)S(1)}, f32[24,128]{1,0:T(8,128)S(1)}) custom-call(f32[4]{0:T(128)} %shifts_hbm.1, f32[8,64,256]{2,1,0:T(8,128)} %rhs.1, f32[13,8,64,256]{3,2,1,0:T(8,128)} %coefs.1), custom_call_target="tpu_custom_call" | custom-call | tf_op jit(solution)/shard_map/basis/pallas_call | solution.py:648
  42.8 2.9 %combine.1 = (f32[5,8,64,256]{3,2,1,0:T(8,128)}, f32[5,5]{1,0:T(8,128)}, f32[8,64,256]{2,1,0:T(8,128)}, f32[8,64,256]{2,1,0:T(8,128)}) custom-call(f32[24,128]{1,0:T(8,128)S(1)} %get-tuple-element.7.gram, f32[5,8,80,256]{3,2,1,0:T(8,128)S(1)} %get-tuple-element.8.v, f32[4,8,80,256]{3,2,1,0:T(8,128)S(1)} %get-tuple-element.9.w), custom_call_target="tpu_custom_call" | custom-call | tf_op jit(solution)/shard_map/combine/pallas_call | solution.py:696

commit v3 on v2

--- a/solution.py
+++ b/solution.py
@@ -37,6 +37,7 @@
     order = steps + 1
     nx, ny, nz = rhs.shape
     tiles = ny // TILE
+    assert tiles >= 4 and nx >= 4 and ny % TILE == 0
     body = slice(PAD, PAD + ny)
     face = (0, nx - 1)
     edge = (0, ny - 1)
@@ -55,9 +56,6 @@
         pltpu.make_async_copy(coefs.at[7:13], weight.at[7:13], load_sem.at[4]),
         pltpu.make_async_copy(shifts_hbm, shifts, load_sem.at[5]),
     ]
-    for load in loads:
-        load.start()
-
     cin[...] = jnp.zeros_like(cin)
 
     barrier = pltpu.get_barrier_semaphore()
@@ -81,6 +79,8 @@
 
     greet(peer(1))
     greet(peer(count - 1))
+    for load in loads:
+        load.start()
     greetings = 4 + 3 * (there[0].astype(jnp.int32) + there[1].astype(jnp.int32))
 
     strides = []
@@ -128,9 +128,15 @@
         )
 
     def y_copy(k, s):
+        kinds = slice(1 if k == 0 else 0, 2)
         return remote(
-            yout.at[k, s], yin.at[k, 1 - s], ys.at[2 * k + s], yr.at[2 * k + 1 - s], {"gy": beside_y[s]}
-        )
+            yout.at[k, s, kinds], yin.at[k, 1 - s, kinds],
+            ys.at[2 * k + s], yr.at[2 * k + 1 - s], {"gy": beside_y[s]},
+        )
+
+    def first_y_copy(s):
+        n, m = 2 * steps + s, 2 * steps + 1 - s
+        return remote(yout.at[0, s, 0], yin.at[0, 1 - s, 0], ys.at[n], yr.at[m], {"gy": beside_y[s]})
 
     def corner_copy(k, sx, sy):
         n, m = 4 * k + 2 * sx + sy, 4 * k + 2 * (1 - sx) + 1 - sy
@@ -138,9 +144,11 @@
             cout.at[n], cin.at[m], cs.at[n], cr.at[m], {"gx": beside_x[sx], "gy": beside_y[sy]}
         )
 
-    def first_copy(s):
+    def first_copy(s, t):
+        n = tiles + 3 + t
         return remote(
-            rhs.at[face[s]], xin.at[0, 1 - s, 0], fs.at[s, tiles + 3], fr.at[1 - s, tiles + 3], {"gx": beside_x[s]}
+            rhs.at[face[s], rows_of(t), :], xin.at[0, 1 - s, 0, rows_of(t), :],
+            fs.at[s, n], fr.at[1 - s, n], {"gx": beside_x[s]},
         )
 
     def far_copy(s, t):
@@ -211,59 +219,63 @@
     def face_a(k, s, t):
         rows = rows_of(t)
         here = slice(PAD + t * TILE, PAD + (t + 1) * TILE)
-        beyond = xin[k, s, 1, rows, :] + far[s, rows, :] * fv[k, face[s], here, :]
+        beyond = xin[k, s, 1, rows, :]
+        if k > 0:
+            beyond = beyond + far[s, rows, :] * fv[k, face[s], here, :]
         if s == 0:
             total = block_a(k, 0, t * TILE, TILE, minus_x=beyond)
         else:
             total = block_a(k, nx - 1, t * TILE, TILE, plus_x=beyond)
         xout[k + 1, s, 0, rows, :] = total
 
-    def start_corners(k):
-        for sy in range(2):
-
-            @pl.when(there[sy])
-            def _():
-                for sx in range(2):
-                    corner_copy(k, sx, sy).start()
-
-    def send_corners(k):
-        for sy in range(2):
+    def stage_corners(k, sy):
+        row = PAD + edge[sy]
+        for sx in range(2):
+            cout[4 * k + 2 * sx + sy, :, :] = fv[k, face[sx], row : row + 1, :]
+
+    def start_corners(k, sy):
+        @pl.when(there[sy])
+        def _():
             for sx in range(2):
-                row = PAD + edge[sy]
-                cout[4 * k + 2 * sx + sy, :, :] = fv[k, face[sx], row : row + 1, :]
-        start_corners(k)
-
-    def send_y(k):
-        for s in range(2):
-            row = PAD + edge[s]
-
-            @pl.when(there[s])
-            def _():
-                for p in range(nx):
-                    yout[k, s, 0, p : p + 1, :] = fv[k, p, row : row + 1, :]
-                    yout[k, s, 1, p : p + 1, :] = fw[k, p, row : row + 1, :]
-                y_copy(k, s).start()
-
-    def finish_edges(k):
-        for sy in range(2):
-
-            @pl.when(there[sy])
-            def _():
-                for sx in range(2):
-                    corner_copy(k, 1 - sx, 1 - sy).wait_recv()
-                y_copy(k, 1 - sy).wait_recv()
-                row = PAD + edge[sy]
-                halo = PAD - 1 if sy == 0 else PAD + ny
-                yin[k, sy, 1, :, :] = yin[k, sy, 1, :, :] + near_row[sy] * yout[k, sy, 0, :, :]
-                yin[k, sy, 0, :, :] = own_row[sy] * yin[k, sy, 0, :, :]
-                for sx in range(2):
-                    p, q = face[sx], edge[sy]
-                    line = cin[4 * k + 2 * sx + sy, :, :]
-                    yin[k, sy, 1, p : p + 1, :] = yin[k, sy, 1, p : p + 1, :] + near_corner[sy, sx : sx + 1, :] * line
+                corner_copy(k, sx, sy).start()
+
+    def stage_y(k, s, kind, fields):
+        row = PAD + edge[s]
+        for p in range(nx):
+            yout[k, s, kind, p : p + 1, :] = fields[k, p, row : row + 1, :]
+
+    def send_y(k, s):
+        @pl.when(there[s])
+        def _():
+            if k > 0:
+                stage_y(k, s, 0, fv)
+            stage_y(k, s, 1, fw)
+            y_copy(k, s).start()
+
+    def own_edge(k, sy):
+        row = PAD + edge[sy]
+        yin[k, sy, 0, :, :] = own_row[sy] * yin[k, sy, 0, :, :]
+        for p in range(nx):
+            fw[k, p, row : row + 1, :] = fw[k, p, row : row + 1, :] + yin[k, sy, 0, p : p + 1, :]
+
+    def finish_edge(k, sy):
+        @pl.when(there[sy])
+        def _():
+            for sx in range(2):
+                corner_copy(k, 1 - sx, 1 - sy).wait_recv()
+            y_copy(k, 1 - sy).wait_recv()
+            halo = PAD - 1 if sy == 0 else PAD + ny
+            yin[k, sy, 1, :, :] = yin[k, sy, 1, :, :] + near_row[sy] * yout[k, sy, 0, :, :]
+            for sx in range(2):
+                p, q = face[sx], edge[sy]
+                line = cin[4 * k + 2 * sx + sy, :, :]
+                yin[k, sy, 1, p : p + 1, :] = yin[k, sy, 1, p : p + 1, :] + near_corner[sy, sx : sx + 1, :] * line
+                if k > 0:
                     xin[k, sx, 1, q : q + 1, :] = xin[k, sx, 1, q : q + 1, :] + far_edge[sx, sy : sy + 1, :] * line
-                for p in range(nx):
-                    fw[k, p, halo : halo + 1, :] = yin[k, sy, 1, p : p + 1, :]
-                    fw[k, p, row : row + 1, :] = fw[k, p, row : row + 1, :] + yin[k, sy, 0, p : p + 1, :]
+            if k > 0:
+                own_edge(k, sy)
+            for p in range(nx):
+                fw[k, p, halo : halo + 1, :] = yin[k, sy, 1, p : p + 1, :]
 
     def products(i, planes, start, size):
         def add(p, totals):
@@ -309,48 +321,51 @@
 
         lax.fori_loop(2, nx - 2, one, 0)
 
-    def edge_m(k):
+    def edge_m(k, sy):
         def one(p, c):
-            block_m(k, p, 0, TILE)
-            block_m(k, p, ny - TILE, TILE)
+            block_m(k, p, (0, ny - TILE)[sy], TILE)
             return c
 
         lax.fori_loop(1, nx - 1, one, 0)
 
-    def edge_a(k):
+    def edge_a(k, sy):
         def one(p, c):
-            block_a(k, p, 0, TILE)
-            block_a(k, p, ny - TILE, TILE)
+            block_a(k, p, (0, ny - TILE)[sy], TILE)
             return c
 
         lax.fori_loop(2, nx - 2, one, 0)
 
     sequence = middle_out(tiles)
+
+    middle = sequence[: tiles // 2]
+    outside = sequence[tiles // 2 :]
 
     loads[0].wait()
     for sy in range(2):
-        for sx in range(2):
-            row = PAD + edge[sy]
-            cout[2 * sx + sy, :, :] = fv[0, face[sx], row : row + 1, :]
+        stage_corners(0, sy)
+        stage_y(0, sy, 0, fv)
     pl.semaphore_wait(barrier, greetings)
+    for t in sequence:
+        for s in range(2):
+            first_copy(s, t).start()
     for s in range(2):
-        first_copy(s).start()
-    start_corners(0)
+        start_corners(0, s)
+
+        @pl.when(there[s])
+        def _():
+            first_y_copy(s).start()
+
     if strides:
         hello_signal(0)
-    loads[1].wait()
-    loads[2].wait()
-    for t in sequence:
+    for t in middle:
         for s in range(2):
-            face_m(0, s, t)
-            x_copy(0, s, t).start()
             far_copy(s, t).start()
-    loads[3].wait()
+    for load in loads[1:4]:
+        load.wait()
     for s in range(2):
         r = edge[s]
         for sy in range(2):
             far_corner[s, sy : sy + 1, :] = weight[3 + sy, face[s], edge[sy] : edge[sy] + 1, :]
-        far_edge_copy(s).start()
         for p in range(nx):
             own_row[s, p : p + 1, :] = weight[3 + s, p, r : r + 1, :]
         for sx in range(2):
@@ -361,8 +376,33 @@
             for copy in near_copies(s):
                 copy.start()
 
-    edge_m(0)
-    send_y(0)
+    for t in sequence:
+        for s in range(2):
+            face_m(0, s, t)
+    for sy in range(2):
+        edge_m(0, sy)
+        send_y(0, sy)
+    for t in sequence:
+        for sy in range(2):
+            if t == (0, tiles - 1)[sy]:
+
+                @pl.when(there[sy])
+                def _():
+                    first_y_copy(1 - sy).wait_recv()
+                    own_edge(0, sy)
+
+        here = slice(PAD + t * TILE, PAD + (t + 1) * TILE)
+        for s in range(2):
+            first_copy(1 - s, t).wait_recv()
+            total = fw[0, face[s], here, :] + weight[1 + s, face[s], rows_of(t), :] * xin[0, s, 0, rows_of(t), :]
+            fw[0, face[s], here, :] = total
+            xout[0, s, 1, rows_of(t), :] = total
+            x_copy(0, s, t).start()
+    for t in outside:
+        for s in range(2):
+            far_copy(s, t).start()
+    for s in range(2):
+        far_edge_copy(s).start()
     inner_m(0)
     loads[4].wait()
     loads[5].wait()
@@ -376,41 +416,37 @@
         if not send:
             forget(k + 1)
             products(k + 1, (2, nx - 2), TILE, ny - 2 * TILE)
-        if k == 0:
-            for s in range(2):
-                first_copy(1 - s).wait_recv()
-        arrived, final, drafted = set(), set(), set()
+        arrived, final = set(), set()
 
         def needs(u):
             return {q for q in (u - 1, u, u + 1) if 0 <= q < tiles}
 
         for t in sequence:
+            sides = [sy for sy in range(2) if t == (0, tiles - 1)[sy]]
+            here = slice(PAD + t * TILE, PAD + (t + 1) * TILE)
             for s in range(2):
                 x_copy(k, 1 - s, t).wait_recv()
-                if k == 0:
+                if k == 1:
                     far_copy(1 - s, t).wait_recv()
-
-                here = slice(PAD + t * TILE, PAD + (t + 1) * TILE)
-                fw[k, face[s], here, :] = (
-                    fw[k, face[s], here, :] + weight[1 + s, face[s], rows_of(t), :] * xin[k, s, 0, rows_of(t), :]
-                )
+                if k > 0:
+                    fw[k, face[s], here, :] = (
+                        fw[k, face[s], here, :]
+                        + weight[1 + s, face[s], rows_of(t), :] * xin[k, s, 0, rows_of(t), :]
+                    )
             arrived.add(t)
-            last = len(arrived) == tiles
-            if last:
-                if k == 0:
+            for sy in sides:
+                if k == 1 and sy == (1 if tiles > 1 else 0):
                     for s in range(2):
                         far_edge_copy(1 - s).wait_recv()
-
-                        @pl.when(there[s])
-                        def _():
-                            for copy in near_copies(1 - s):
-                                copy.wait_recv()
-
-                finish_edges(k)
-            ready = [
-                u for u in sequence
-                if u not in final and needs(u) <= arrived and (last or 0 < u < tiles - 1)
-            ]
+                if k == 0:
+
+                    @pl.when(there[sy])
+                    def _():
+                        for copy in near_copies(1 - sy):
+                            copy.wait_recv()
+
+                finish_edge(k, sy)
+            ready = [u for u in sequence if u not in final and needs(u) <= arrived]
             for u in ready:
                 final.add(u)
             extra = sorted(set().union(*[needs(u) for u in ready]) - final) if send and ready else []
@@ -421,22 +457,25 @@
                 block_a(k, 1, u * TILE, TILE)
                 block_a(k, nx - 2, u * TILE, TILE)
             if send:
-                if last:
-                    send_corners(k + 1)
+                for sy in sides:
+                    stage_corners(k + 1, sy)
+                    start_corners(k + 1, sy)
                 for u in ready:
                     for s in range(2):
                         face_m(k + 1, s, u)
                         x_copy(k + 1, s, u).start()
-        edge_a(k)
+            for sy in sides:
+                edge_a(k, sy)
+                if send:
+                    edge_m(k + 1, sy)
+                    send_y(k + 1, sy)
+                else:
+                    products(k + 1, (2, nx - 2), (0, ny - TILE)[sy], TILE)
         if send:
-            edge_m(k + 1)
-            send_y(k + 1)
             inner_m(k + 1)
 
     for k in range(steps):
         step(k, k + 1 < steps)
-    products(steps, (2, nx - 2), 0, TILE)
-    products(steps, (2, nx - 2), ny - TILE, TILE)
     products(steps, (0, 2), 0, ny)
     products(steps, (nx - 2, nx), 0, ny)
     keep(steps)
@@ -477,13 +516,14 @@
                     corner_copy(k, sx, s).wait_send()
 
     for s in range(2):
-        first_copy(s).wait_send()
         for t in range(tiles):
+            first_copy(s, t).wait_send()
             far_copy(s, t).wait_send()
         far_edge_copy(s).wait_send()
 
         @pl.when(there[s])
         def _():
+            first_y_copy(s).wait_send()
             for copy in near_copies(s):
                 copy.wait_send()
 
@@ -560,7 +600,7 @@
     return factor, inverse, weights, combine
 
 
-def combine_kernel(cells, gram, v, w, basis, factor_out, solution_out, residual, table, basis_v, sol_v, res_v, sem):
+def combine_kernel(cells, gram, v, w, basis, factor_out, solution_out, residual, table, basis_v, sol_v, res_v, factor_v, sem, factor_sem):
     order, nx, ny, nz = basis_v.shape
     steps = order - 1
     pairs = [(j, k) for k in range(order) for j in range(k + 1)]
@@ -575,7 +615,9 @@
     whole = jnp.zeros((8, ROWS), jnp.float32)
     for (i, j), value in factor.items():
         whole = jnp.where((row == i) & (column == j), value, whole)
-    factor_out[...] = whole[:order, :order]
+    factor_v[...] = whole[:order, :order]
+    factor_copy = pltpu.make_async_copy(factor_v, factor_out, factor_sem)
+    factor_copy.start()
 
     def mul(n, x):
         return table[n][None] * x
@@ -628,6 +670,7 @@
 
     lax.fori_loop(0, nx, plane, 0)
     lax.fori_loop(0, nx, finish, 0)
+    factor_copy.wait()
 
 
 def device_body(n_gx, n_gy, rhs, coefs, shifts):
@@ -677,12 +720,12 @@
             pltpu.SemaphoreType.REGULAR((16,)),
             dma((2 * steps * tiles,)),
             dma((2 * steps * tiles,)),
-            dma((2 * steps,)),
-            dma((2 * steps,)),
+            dma((2 * steps + 2,)),
+            dma((2 * steps + 2,)),
             dma((4 * steps,)),
             dma((4 * steps,)),
-            dma((2, tiles + 4)),
-            dma((2, tiles + 4)),
+            dma((2, 2 * tiles + 3)),
+            dma((2, 2 * tiles + 3)),
             dma((n_gx * n_gy,)),
             dma((n_gx * n_gy,)),
         ],
@@ -702,13 +745,15 @@
             jax.ShapeDtypeStruct((nx, ny, nz), f32),
         ),
         in_specs=[vmem, vmem, vmem],
-        out_specs=(hbm, vmem, hbm, hbm),
+        out_specs=(hbm, hbm, hbm, hbm),
         scratch_shapes=[
             pltpu.VMEM((order * (order + 1) // 2 + steps + order, 8, ROWS), f32),
             pltpu.VMEM((order, nx, ny, nz), f32),
             pltpu.VMEM((nx, ny, nz), f32),
             pltpu.VMEM((nx, ny, nz), f32),
+            pltpu.VMEM((order, order), f32),
             dma((nx, 3)),
+            dma,
         ],
         compiler_params=pltpu.CompilerParams(vmem_limit_bytes=32 * 2**20),
         name="combine",

time: 45.9 us -> 47.1 us (1.026)
  Pallas kernels: 45.1 us -> 46.4 us
    pallas_call x1, Pallas kernels: 42.2 us -> 44.1 us  [device_body(): pl.pallas_call(functools.partial(basis_kernel, n_gx, n_gy), out_shape=(ja...]
    pallas_call x1, Pallas kernels: 2.87 us -> 2.3 us  [device_body(): pl.pallas_call(functools.partial(combine_kernel, cells), out_shape=(jax.S...]
where the time goes in v3:
time: 47.1 us; the launch traced here: 47 us
  Pallas kernels  46.4 us (99%)
  between operations  0.64 us (1%)
    pallas_call x1, Pallas kernels, device_body(): pl.pallas_call(functools.partial(basis_kernel, n_gx, n_gy), out_shape=(ja...  44.1 us
    pallas_call x1, Pallas kernels, device_body(): pl.pallas_call(functools.partial(combine_kernel, cells), out_shape=(jax.S...  2.3 us

profile of v3, /device:TPU:0, one launch (start us, length us, event | category | flops | bytes accessed | tf_op | source)
XLA Modules:
  0.0 47.0 jit_solution(15620765787302415136)
XLA Ops:
  0.6 44.1 %basis.1 = (f32[5,8,80,256]{3,2,1,0:T(8,128)S(1)}, f32[4,8,80,256]{3,2,1,0:T(8,128)S(1)}, f32[24,128]{1,0:T(8,128)S(1)}) custom-call(f32[4]{0:T(128)} %shifts_hbm.1, f32[8,64,256]{2,1,0:T(8,128)} %rhs.1, f32[13,8,64,256]{3,2,1,0:T(8,128)} %coefs.1), custom_call_target="tpu_custom_call" | custom-call | tf_op jit(solution)/shard_map/basis/pallas_call | solution.py:691
  44.7 2.3 %combine.1 = (f32[5,8,64,256]{3,2,1,0:T(8,128)}, f32[5,5]{1,0:T(8,128)}, f32[8,64,256]{2,1,0:T(8,128)}, f32[8,64,256]{2,1,0:T(8,128)}) custom-call(f32[24,128]{1,0:T(8,128)S(1)} %get-tuple-element.7.gram, f32[5,8,80,256]{3,2,1,0:T(8,128)S(1)} %get-tuple-element.8.v, f32[4,8,80,256]{3,2,1,0:T(8,128)S(1)} %get-tuple-element.9.w), custom_call_target="tpu_custom_call" | custom-call | tf_op jit(solution)/shard_map/combine/pallas_call | solution.py:739

commit v4 on v3

--- a/solution.py
+++ b/solution.py
@@ -128,15 +128,9 @@
         )
 
     def y_copy(k, s):
-        kinds = slice(1 if k == 0 else 0, 2)
         return remote(
-            yout.at[k, s, kinds], yin.at[k, 1 - s, kinds],
-            ys.at[2 * k + s], yr.at[2 * k + 1 - s], {"gy": beside_y[s]},
-        )
-
-    def first_y_copy(s):
-        n, m = 2 * steps + s, 2 * steps + 1 - s
-        return remote(yout.at[0, s, 0], yin.at[0, 1 - s, 0], ys.at[n], yr.at[m], {"gy": beside_y[s]})
+            yout.at[k, s], yin.at[k, 1 - s], ys.at[2 * k + s], yr.at[2 * k + 1 - s], {"gy": beside_y[s]}
+        )
 
     def corner_copy(k, sx, sy):
         n, m = 4 * k + 2 * sx + sy, 4 * k + 2 * (1 - sx) + 1 - sy
@@ -144,11 +138,10 @@
             cout.at[n], cin.at[m], cs.at[n], cr.at[m], {"gx": beside_x[sx], "gy": beside_y[sy]}
         )
 
-    def first_copy(s, t):
-        n = tiles + 3 + t
+    def first_copy(s):
+        n = tiles + 3
         return remote(
-            rhs.at[face[s], rows_of(t), :], xin.at[0, 1 - s, 0, rows_of(t), :],
-            fs.at[s, n], fr.at[1 - s, n], {"gx": beside_x[s]},
+            rhs.at[face[s]], xin.at[0, 1 - s, 0], fs.at[s, n], fr.at[1 - s, n], {"gx": beside_x[s]}
         )
 
     def far_copy(s, t):
@@ -219,9 +212,7 @@
     def face_a(k, s, t):
         rows = rows_of(t)
         here = slice(PAD + t * TILE, PAD + (t + 1) * TILE)
-        beyond = xin[k, s, 1, rows, :]
-        if k > 0:
-            beyond = beyond + far[s, rows, :] * fv[k, face[s], here, :]
+        beyond = xin[k, s, 1, rows, :] + far[s, rows, :] * fv[k, face[s], here, :]
         if s == 0:
             total = block_a(k, 0, t * TILE, TILE, minus_x=beyond)
         else:
@@ -247,8 +238,7 @@
     def send_y(k, s):
         @pl.when(there[s])
         def _():
-            if k > 0:
-                stage_y(k, s, 0, fv)
+            stage_y(k, s, 0, fv)
             stage_y(k, s, 1, fw)
             y_copy(k, s).start()
 
@@ -270,10 +260,8 @@
                 p, q = face[sx], edge[sy]
                 line = cin[4 * k + 2 * sx + sy, :, :]
                 yin[k, sy, 1, p : p + 1, :] = yin[k, sy, 1, p : p + 1, :] + near_corner[sy, sx : sx + 1, :] * line
-                if k > 0:
-                    xin[k, sx, 1, q : q + 1, :] = xin[k, sx, 1, q : q + 1, :] + far_edge[sx, sy : sy + 1, :] * line
-            if k > 0:
-                own_edge(k, sy)
+                xin[k, sx, 1, q : q + 1, :] = xin[k, sx, 1, q : q + 1, :] + far_edge[sx, sy : sy + 1, :] * line
+            own_edge(k, sy)
             for p in range(nx):
                 fw[k, p, halo : halo + 1, :] = yin[k, sy, 1, p : p + 1, :]
 
@@ -337,35 +325,31 @@
 
     sequence = middle_out(tiles)
 
-    middle = sequence[: tiles // 2]
-    outside = sequence[tiles // 2 :]
 
     loads[0].wait()
     for sy in range(2):
         stage_corners(0, sy)
-        stage_y(0, sy, 0, fv)
     pl.semaphore_wait(barrier, greetings)
+    for s in range(2):
+        first_copy(s).start()
+    for s in range(2):
+        start_corners(0, s)
+    if strides:
+        hello_signal(0)
+    loads[1].wait()
+    loads[2].wait()
     for t in sequence:
         for s in range(2):
-            first_copy(s, t).start()
+            face_m(0, s, t)
+            x_copy(0, s, t).start()
+            far_copy(s, t).start()
     for s in range(2):
-        start_corners(0, s)
-
-        @pl.when(there[s])
-        def _():
-            first_y_copy(s).start()
-
-    if strides:
-        hello_signal(0)
-    for t in middle:
-        for s in range(2):
-            far_copy(s, t).start()
-    for load in loads[1:4]:
-        load.wait()
+        for sy in range(2):
+            far_corner[s, sy : sy + 1, :] = weight[3 + sy, face[s], edge[sy] : edge[sy] + 1, :]
+        far_edge_copy(s).start()
+    loads[3].wait()
     for s in range(2):
         r = edge[s]
-        for sy in range(2):
-            far_corner[s, sy : sy + 1, :] = weight[3 + sy, face[s], edge[sy] : edge[sy] + 1, :]
         for p in range(nx):
             own_row[s, p : p + 1, :] = weight[3 + s, p, r : r + 1, :]
         for sx in range(2):
@@ -376,33 +360,8 @@
             for copy in near_copies(s):
                 copy.start()
 
-    for t in sequence:
-        for s in range(2):
-            face_m(0, s, t)
-    for sy in range(2):
-        edge_m(0, sy)
-        send_y(0, sy)
-    for t in sequence:
-        for sy in range(2):
-            if t == (0, tiles - 1)[sy]:
-
-                @pl.when(there[sy])
-                def _():
-                    first_y_copy(1 - sy).wait_recv()
-                    own_edge(0, sy)
-
-        here = slice(PAD + t * TILE, PAD + (t + 1) * TILE)
-        for s in range(2):
-            first_copy(1 - s, t).wait_recv()
-            total = fw[0, face[s], here, :] + weight[1 + s, face[s], rows_of(t), :] * xin[0, s, 0, rows_of(t), :]
-            fw[0, face[s], here, :] = total
-            xout[0, s, 1, rows_of(t), :] = total
-            x_copy(0, s, t).start()
-    for t in outside:
-        for s in range(2):
-            far_copy(s, t).start()
-    for s in range(2):
-        far_edge_copy(s).start()
+        edge_m(0, s)
+        send_y(0, s)
     inner_m(0)
     loads[4].wait()
     loads[5].wait()
@@ -422,20 +381,20 @@
             return {q for q in (u - 1, u, u + 1) if 0 <= q < tiles}
 
         for t in sequence:
-            sides = [sy for sy in range(2) if t == (0, tiles - 1)[sy]]
+            sides = [1, 0] if t == sequence[-1] else []
             here = slice(PAD + t * TILE, PAD + (t + 1) * TILE)
             for s in range(2):
                 x_copy(k, 1 - s, t).wait_recv()
-                if k == 1:
+                if k == 0:
+                    if t == sequence[0]:
+                        first_copy(1 - s).wait_recv()
                     far_copy(1 - s, t).wait_recv()
-                if k > 0:
-                    fw[k, face[s], here, :] = (
-                        fw[k, face[s], here, :]
-                        + weight[1 + s, face[s], rows_of(t), :] * xin[k, s, 0, rows_of(t), :]
-                    )
+                fw[k, face[s], here, :] = (
+                    fw[k, face[s], here, :] + weight[1 + s, face[s], rows_of(t), :] * xin[k, s, 0, rows_of(t), :]
+                )
             arrived.add(t)
             for sy in sides:
-                if k == 1 and sy == (1 if tiles > 1 else 0):
+                if k == 0 and sy == sides[0]:
                     for s in range(2):
                         far_edge_copy(1 - s).wait_recv()
                 if k == 0:
@@ -446,7 +405,10 @@
                             copy.wait_recv()
 
                 finish_edge(k, sy)
-            ready = [u for u in sequence if u not in final and needs(u) <= arrived]
+            ready = [
+                u for u in sequence
+                if u not in final and needs(u) <= arrived and (sides or 0 < u < tiles - 1)
+            ]
             for u in ready:
                 final.add(u)
             extra = sorted(set().union(*[needs(u) for u in ready]) - final) if send and ready else []
@@ -487,22 +449,20 @@
     packed = jnp.sum(jnp.where(row == lane, jnp.broadcast_to(column, row.shape), 0.0), axis=0, keepdims=True)
     peers[pl.ds(me, 1), :] = packed
 
-    def peer_copy(d):
-        return remote(peers.at[pl.ds(me, 1), :], peers.at[pl.ds(me, 1), :], gs.at[d], gr.at[d], peer(d))
-
-    def peer_start(d, c):
-        peer_copy(d).start()
-        return c
-
-    def peer_arrive(d, c):
-        peer_copy(d).wait_recv()
-        return c
-
-    def peer_sent(d, c):
-        peer_copy(d).wait_send()
-        return c
-
-    lax.fori_loop(1, count, peer_start, 0)
+    low_half = gx < n_gx // 2
+
+    def peer_copy(j):
+        down, up = count - 1 - j, j
+        other = jnp.where(low_half, jnp.where(down > me, down, down - 1), jnp.where(up < me, up, up + 1))
+        device = {"gx": lax.div(other, n_gy), "gy": lax.rem(other, n_gy)}
+        return remote(peers.at[pl.ds(me, 1), :], peers.at[pl.ds(me, 1), :], gs.at[0], gr.at[0], device)
+
+    for j in range(count - 1):
+        peer_copy(j).start()
+
+    def all_peers():
+        rows = pl.ds(0, count - 1)
+        return remote(peers.at[rows, :], peers.at[rows, :], gs.at[0], gr.at[0], peer(1))
 
     for k in range(steps):
         for s in range(2):
@@ -516,24 +476,23 @@
                     corner_copy(k, sx, s).wait_send()
 
     for s in range(2):
+        first_copy(s).wait_send()
         for t in range(tiles):
-            first_copy(s, t).wait_send()
             far_copy(s, t).wait_send()
         far_edge_copy(s).wait_send()
 
         @pl.when(there[s])
         def _():
-            first_y_copy(s).wait_send()
             for copy in near_copies(s):
                 copy.wait_send()
 
-    lax.fori_loop(1, count, peer_arrive, 0)
+    all_peers().wait_recv()
     total = jnp.sum(peers[...], axis=0, keepdims=True)
     spread = jnp.sum(jnp.where(row == lane, jnp.broadcast_to(total, row.shape), 0.0), axis=1, keepdims=True)
     gram[0:height, :] = jnp.broadcast_to(spread, row.shape)
     for k in range(steps):
         gram[height + k : height + k + 1, :] = jnp.full((1, ROWS), shifts[k], jnp.float32)
-    lax.fori_loop(1, count, peer_sent, 0)
+    all_peers().wait_send()
 
 
 def small_algebra(gram, steps, cells):
@@ -720,14 +679,14 @@
             pltpu.SemaphoreType.REGULAR((16,)),
             dma((2 * steps * tiles,)),
             dma((2 * steps * tiles,)),
-            dma((2 * steps + 2,)),
-            dma((2 * steps + 2,)),
+            dma((2 * steps,)),
+            dma((2 * steps,)),
             dma((4 * steps,)),
             dma((4 * steps,)),
             dma((2, 2 * tiles + 3)),
             dma((2, 2 * tiles + 3)),
-            dma((n_gx * n_gy,)),
-            dma((n_gx * n_gy,)),
+            dma((1,)),
+            dma((1,)),
         ],
         compiler_params=pltpu.CompilerParams(
             collective_id=0, has_side_effects=True, vmem_limit_bytes=32 * 2**20

time: 47.1 us -> 44.5 us (0.945)
  Pallas kernels: 46.4 us -> 43.8 us
    pallas_call x1, Pallas kernels: 44.1 us -> 41.5 us  [device_body(): pl.pallas_call(functools.partial(basis_kernel, n_gx, n_gy), out_shape=(ja...]
where the time goes in v4:
time: 44.5 us; the launch traced here: 44.4 us
  Pallas kernels  43.8 us (98%)
  between operations  0.64 us (1%)
    pallas_call x1, Pallas kernels, device_body(): pl.pallas_call(functools.partial(basis_kernel, n_gx, n_gy), out_shape=(ja...  41.5 us
    pallas_call x1, Pallas kernels, device_body(): pl.pallas_call(functools.partial(combine_kernel, cells), out_shape=(jax.S...  2.3 us

profile of v4, /device:TPU:0, one launch (start us, length us, event | category | flops | bytes accessed | tf_op | source)
XLA Modules:
  0.0 44.4 jit_solution(9017972017843857854)
XLA Ops:
  0.6 41.5 %basis.1 = (f32[5,8,80,256]{3,2,1,0:T(8,128)S(1)}, f32[4,8,80,256]{3,2,1,0:T(8,128)S(1)}, f32[24,128]{1,0:T(8,128)S(1)}) custom-call(f32[4]{0:T(128)} %shifts_hbm.1, f32[8,64,256]{2,1,0:T(8,128)} %rhs.1, f32[13,8,64,256]{3,2,1,0:T(8,128)} %coefs.1), custom_call_target="tpu_custom_call" | custom-call | tf_op jit(solution)/shard_map/basis/pallas_call | solution.py:650
  42.1 2.3 %combine.1 = (f32[5,8,64,256]{3,2,1,0:T(8,128)}, f32[5,5]{1,0:T(8,128)}, f32[8,64,256]{2,1,0:T(8,128)}, f32[8,64,256]{2,1,0:T(8,128)}) custom-call(f32[24,128]{1,0:T(8,128)S(1)} %get-tuple-element.7.gram, f32[5,8,80,256]{3,2,1,0:T(8,128)S(1)} %get-tuple-element.8.v, f32[4,8,80,256]{3,2,1,0:T(8,128)S(1)} %get-tuple-element.9.w), custom_call_target="tpu_custom_call" | custom-call | tf_op jit(solution)/shard_map/combine/pallas_call | solution.py:698

commit v5 on v4

--- a/solution.py
+++ b/solution.py
@@ -326,27 +326,27 @@
     sequence = middle_out(tiles)
 
 
+    pl.semaphore_wait(barrier, greetings)
+    for s in range(2):
+        first_copy(s).start()
     loads[0].wait()
     for sy in range(2):
         stage_corners(0, sy)
-    pl.semaphore_wait(barrier, greetings)
-    for s in range(2):
-        first_copy(s).start()
     for s in range(2):
         start_corners(0, s)
     if strides:
         hello_signal(0)
     loads[1].wait()
     loads[2].wait()
+    for s in range(2):
+        for sy in range(2):
+            far_corner[s, sy : sy + 1, :] = weight[3 + sy, face[s], edge[sy] : edge[sy] + 1, :]
+        far_edge_copy(s).start()
     for t in sequence:
         for s in range(2):
             face_m(0, s, t)
             x_copy(0, s, t).start()
             far_copy(s, t).start()
-    for s in range(2):
-        for sy in range(2):
-            far_corner[s, sy : sy + 1, :] = weight[3 + sy, face[s], edge[sy] : edge[sy] + 1, :]
-        far_edge_copy(s).start()
     loads[3].wait()
     for s in range(2):
         r = edge[s]
@@ -365,6 +365,8 @@
     inner_m(0)
     loads[4].wait()
     loads[5].wait()
+
+    final_at = (sequence[-1], sequence[-1])
 
     def step(k, send):
         inner_a(k)
@@ -380,8 +382,25 @@
         def needs(u):
             return {q for q in (u - 1, u, u + 1) if 0 <= q < tiles}
 
+        def advance(ready, corners):
+            final.update(ready)
+            drafts = sorted(set().union(*[needs(u) for u in ready]) - final) if send else []
+            for s in range(2):
+                for u in ready + drafts:
+                    face_a(k, s, u)
+            for u in ready:
+                for s in range(2):
+                    block_a(k, (1, nx - 2)[s], u * TILE, TILE)
+            if send:
+                for sy in corners:
+                    stage_corners(k + 1, sy)
+                    start_corners(k + 1, sy)
+                for u in ready:
+                    for s in range(2):
+                        face_m(k + 1, s, u)
+                        x_copy(k + 1, s, u).start()
+
         for t in sequence:
-            sides = [1, 0] if t == sequence[-1] else []
             here = slice(PAD + t * TILE, PAD + (t + 1) * TILE)
             for s in range(2):
                 x_copy(k, 1 - s, t).wait_recv()
@@ -393,11 +412,13 @@
                     fw[k, face[s], here, :] + weight[1 + s, face[s], rows_of(t), :] * xin[k, s, 0, rows_of(t), :]
                 )
             arrived.add(t)
-            for sy in sides:
-                if k == 0 and sy == sides[0]:
-                    for s in range(2):
-                        far_edge_copy(1 - s).wait_recv()
+            ready = [u for u in sequence if u not in final and needs(u) <= arrived and 0 < u < tiles - 1]
+            ends = [sy for sy in (1, 0) if t == final_at[sy]]
+            for sy in ends:
                 if k == 0:
+                    if sy == 1:
+                        for s in range(2):
+                            far_edge_copy(1 - s).wait_recv()
 
                     @pl.when(there[sy])
                     def _():
@@ -405,41 +426,27 @@
                             copy.wait_recv()
 
                 finish_edge(k, sy)
-            ready = [
-                u for u in sequence
-                if u not in final and needs(u) <= arrived and (sides or 0 < u < tiles - 1)
-            ]
-            for u in ready:
-                final.add(u)
-            extra = sorted(set().union(*[needs(u) for u in ready]) - final) if send and ready else []
-            for u in ready + extra:
-                for s in range(2):
-                    face_a(k, s, u)
-            for u in ready:
-                block_a(k, 1, u * TILE, TILE)
-                block_a(k, nx - 2, u * TILE, TILE)
+                ready.append((0, tiles - 1)[sy])
+            if ready:
+                advance(ready, ends)
+            if not send and t == sequence[-2]:
+                for planes in ((0, 2), (nx - 2, nx)):
+                    products(k + 1, planes, 2 * TILE, ny - 4 * TILE)
+        for sy in (1, 0):
+            edge_a(k, sy)
             if send:
-                for sy in sides:
-                    stage_corners(k + 1, sy)
-                    start_corners(k + 1, sy)
-                for u in ready:
-                    for s in range(2):
-                        face_m(k + 1, s, u)
-                        x_copy(k + 1, s, u).start()
-            for sy in sides:
-                edge_a(k, sy)
-                if send:
-                    edge_m(k + 1, sy)
-                    send_y(k + 1, sy)
-                else:
-                    products(k + 1, (2, nx - 2), (0, ny - TILE)[sy], TILE)
+                edge_m(k + 1, sy)
+                send_y(k + 1, sy)
+            else:
+                products(k + 1, (2, nx - 2), (0, ny - TILE)[sy], TILE)
         if send:
             inner_m(k + 1)
 
     for k in range(steps):
         step(k, k + 1 < steps)
-    products(steps, (0, 2), 0, ny)
-    products(steps, (nx - 2, nx), 0, ny)
+    for planes in ((0, 2), (nx - 2, nx)):
+        for start in (0, ny - 2 * TILE):
+            products(steps, planes, start, 2 * TILE)
     keep(steps)
 
     height = part.shape[0]

time: 44.5 us -> 44.6 us (level)
  no operation moved by 1% of the time
where the time goes in v5:
time: 44.6 us; the launch traced here: 44.4 us
  Pallas kernels  43.8 us (98%)
  between operations  0.64 us (1%)
    pallas_call x1, Pallas kernels, device_body(): pl.pallas_call(functools.partial(basis_kernel, n_gx, n_gy), out_shape=(ja...  41.5 us
    pallas_call x1, Pallas kernels, device_body(): pl.pallas_call(functools.partial(combine_kernel, cells), out_shape=(jax.S...  2.3 us

profile of v5, /device:TPU:0, one launch (start us, length us, event | category | flops | bytes accessed | tf_op | source)
XLA Modules:
  0.0 44.4 jit_solution(6751155298249276486)
XLA Ops:
  0.6 41.5 %basis.1 = (f32[5,8,80,256]{3,2,1,0:T(8,128)S(1)}, f32[4,8,80,256]{3,2,1,0:T(8,128)S(1)}, f32[24,128]{1,0:T(8,128)S(1)}) custom-call(f32[4]{0:T(128)} %shifts_hbm.1, f32[8,64,256]{2,1,0:T(8,128)} %rhs.1, f32[13,8,64,256]{3,2,1,0:T(8,128)} %coefs.1), custom_call_target="tpu_custom_call" | custom-call | tf_op jit(solution)/shard_map/basis/pallas_call | solution.py:657
  42.1 2.3 %combine.1 = (f32[5,8,64,256]{3,2,1,0:T(8,128)}, f32[5,5]{1,0:T(8,128)}, f32[8,64,256]{2,1,0:T(8,128)}, f32[8,64,256]{2,1,0:T(8,128)}) custom-call(f32[24,128]{1,0:T(8,128)S(1)} %get-tuple-element.7.gram, f32[5,8,80,256]{3,2,1,0:T(8,128)S(1)} %get-tuple-element.8.v, f32[4,8,80,256]{3,2,1,0:T(8,128)S(1)} %get-tuple-element.9.w), custom_call_target="tpu_custom_call" | custom-call | tf_op jit(solution)/shard_map/combine/pallas_call | solution.py:705
